TPU v7x, 32 devices: a whole 2x2x4 slice. The times are simulated.
32 devices in a mesh: dp: 4 (over x, core), fsdp: 8 (over z, y).
Axes of the slice: x: 2, y: 2, z: 4, core: 2. Of those that a mesh axis runs over, the one named last changes fastest.
Arguments:
- tokens: bfloat16 [8, 1024, 768], P('dp', 'fsdp'), may hold values from -6 to 6
- seg_ids: int32 [8, 1024], P('dp'), may hold values from 0 to 7, never falling along the last dimension, each value on 1 to 768 neighbouring positions
- token_types: int32 [8, 1024], P('dp'), may hold values from 0 to 1
- attn_in: bfloat16 [768, 2304], P(('dp', 'fsdp')), may hold values from -0.21875 to 0.21875
- attn_out: bfloat16 [768, 768], P(('dp', 'fsdp')), may hold values from -0.875 to 0.875
- pos_kernel: bfloat16 [768, 768], P(('dp', 'fsdp')), may hold values from -0.375 to 0.375
- ffn_in: bfloat16 [768, 3072], P(('dp', 'fsdp')), may hold values from -0.21875 to 0.21875
- ffn_out: bfloat16 [3072, 768], P(('dp', 'fsdp')), may hold values from -0.109375 to 0.109375
- head_vectors: bfloat16 [5, 768], P(None, ('dp', 'fsdp')), may hold values from -3 to 3
- norm_gains: bfloat16 [2, 768], P(None, ('dp', 'fsdp')), may hold values from 0.5 to 1.5
- norm_shifts: bfloat16 [2, 768], P(None, ('dp', 'fsdp')), may hold values from -3 to 3
- out_bias: bfloat16 [2, 768], P(None, ('dp', 'fsdp')), may hold values from -3 to 3
- ffn_bias: bfloat16 [3072], P(('dp', 'fsdp')), may hold values from -3 to 3
- cotangent: bfloat16 [8, 1024, 768], P('dp', 'fsdp'), may hold values from -6 to 6
Outputs:
- output: bfloat16 [8, 1024, 768], P('dp', 'fsdp')
- input_grad: float32 [8, 1024, 768], P('dp', 'fsdp')
- grad_attn_in: float32 [768, 2304], P(('dp', 'fsdp'))
- grad_attn_out: float32 [768, 768], P(('dp', 'fsdp'))
- grad_pos_kernel: float32 [768, 768], P(('dp', 'fsdp'))
- grad_ffn_in: float32 [768, 3072], P(('dp', 'fsdp'))
- grad_ffn_out: float32 [3072, 768], P(('dp', 'fsdp'))
- grad_head_vectors: float32 [5, 768], P(None, ('dp', 'fsdp'))
- grad_norm_gains: float32 [2, 768], P(None, ('dp', 'fsdp'))
- grad_norm_shifts: float32 [2, 768], P(None, ('dp', 'fsdp'))
- grad_out_bias: float32 [2, 768], P(None, ('dp', 'fsdp'))
- grad_ffn_bias: float32 [3072], P(('dp', 'fsdp'))
Inputs may be any that keep to these rules, and one draw needn't show every extreme that they name: `seg_ids`: in each sequence the document numbers never fall; every document has 1 to 768 positions and one has exactly 768; a position attends only to positions of its own document.
All inputs are finite; a program needn't handle non-finite values.
Results may differ from a plain program's by a relative error of at most 0.017.
Values may be sent and summed in bfloat16 or wider, within the bound.
A program may use at most 192 MiB of HBM per device.

v0:
```python
import jax
import jax.numpy as jnp
from jax import lax
from jax.sharding import PartitionSpec as P

D = 768
H = 12
DH = 64
FF = 3072
HD = 768


EPSILON = 1e-06
HIGHEST_PREC = lax.Precision.HIGHEST


def gelu_tanh(values):
    return (
        0.5
        * values
        * (1.0 + jnp.tanh(0.7978845608028654 * (values + 0.044715 * values * values * values)))
    )


def angle_tables(positions, width):
    half_width = width // 2
    freq_index = jnp.arange(half_width, dtype=jnp.float32)
    inverse = jnp.power(10000.0, -freq_index / half_width)
    angles = positions[:, None] * inverse[None, :]
    return (jnp.sin(angles), jnp.cos(angles))


def layer_norm(values, gain, shift):
    center = values - jnp.mean(values, axis=-1, keepdims=True)
    inv_std = lax.rsqrt(jnp.mean(center * center, axis=-1, keepdims=True) + EPSILON)
    normed = center * inv_std
    return (normed * gain + shift, normed, inv_std)


def norm_back(grad_out, normed, inv_std, gain):
    grad_norm = grad_out * gain
    return inv_std * (
        grad_norm
        - jnp.mean(grad_norm, axis=-1, keepdims=True)
        - normed * jnp.mean(grad_norm * normed, axis=-1, keepdims=True)
    )


def fetch_forward(shards):
    return (
        lax.all_gather(shards[0], ("dp", "fsdp"), axis=0, tiled=True),
        lax.all_gather(shards[1], ("dp", "fsdp"), axis=0, tiled=True),
        lax.all_gather(shards[2], ("dp", "fsdp"), axis=0, tiled=True),
        lax.all_gather(shards[3], ("dp", "fsdp"), axis=0, tiled=True),
        lax.all_gather(shards[4], ("dp", "fsdp"), axis=0, tiled=True),
        lax.all_gather(shards[5], ("dp", "fsdp"), axis=1, tiled=True),
        lax.all_gather(shards[6], ("dp", "fsdp"), axis=1, tiled=True),
        lax.all_gather(shards[7], ("dp", "fsdp"), axis=1, tiled=True),
        lax.all_gather(shards[8], ("dp", "fsdp"), axis=1, tiled=True),
        lax.all_gather(shards[9], ("dp", "fsdp"), axis=0, tiled=True),
    )


def fetch_backward(shards):
    return (
        lax.all_gather(shards[0], ("dp", "fsdp"), axis=0, tiled=True),
        lax.all_gather(shards[1], ("dp", "fsdp"), axis=0, tiled=True),
        lax.all_gather(shards[2], ("dp", "fsdp"), axis=0, tiled=True),
        lax.all_gather(shards[3], ("dp", "fsdp"), axis=0, tiled=True),
        lax.all_gather(shards[4], ("dp", "fsdp"), axis=0, tiled=True),
        lax.all_gather(shards[5], ("dp", "fsdp"), axis=1, tiled=True),
        lax.all_gather(shards[6], ("dp", "fsdp"), axis=1, tiled=True),
        lax.all_gather(shards[7], ("dp", "fsdp"), axis=1, tiled=True),
        lax.all_gather(shards[8], ("dp", "fsdp"), axis=1, tiled=True),
        lax.all_gather(shards[9], ("dp", "fsdp"), axis=0, tiled=True),
    )


def score_block(q_content, q_rel, type_terms, keys3, k_rel, same_type):
    content = jnp.einsum("rhe,jhe->rhj", q_content, keys3, preferred_element_type=jnp.float32)
    position = jnp.einsum("rhc,jc->rhj", q_rel, k_rel, preferred_element_type=jnp.float32)
    typed = jnp.where(same_type, type_terms[:, :, 1:2], type_terms[:, :, 0:1])
    return DH ** (-0.5) * (content + position + typed)


def relative_queries(q_pos, w_pos, positions):
    proj_pos = jnp.einsum(
        "rhe,che->rhc", q_pos, w_pos.reshape(D, H, DH), preferred_element_type=jnp.float32
    )
    sines, cosines = angle_tables(positions, D)
    sin_q = sines[:, None, :]
    cos_q = cosines[:, None, :]
    half_width = D // 2
    pos_sin = proj_pos[..., :half_width]
    pos_cos = proj_pos[..., half_width:]
    q_rel = jnp.concatenate(
        [pos_sin * sin_q + pos_cos * cos_q, pos_cos * sin_q - pos_sin * cos_q], axis=-1
    ).astype(jnp.bfloat16)
    return (q_rel, sin_q, cos_q)


def forward_micro(weights, x_rows, seg_row, type_row, start, k_rel):
    w_in, w_out, w_pos, w_up, w_down, head_vec, gains, shifts, biases, up_bias = weights
    row_count = x_rows.shape[0]
    head_f = head_vec.astype(jnp.float32)
    gains_f = gains.astype(jnp.float32)
    shifts_f = shifts.astype(jnp.float32)
    biases_f = biases.astype(jnp.float32)
    proj = jnp.dot(x_rows, w_in, preferred_element_type=jnp.float32)
    query = proj[:, :HD]
    key_local = proj[:, HD : 2 * HD].astype(jnp.bfloat16)
    value_local = proj[:, 2 * HD :].astype(jnp.bfloat16)
    keys, values = (
        lax.all_gather(key_local, "fsdp", axis=0, tiled=True),
        lax.all_gather(value_local, "fsdp", axis=0, tiled=True),
    )
    keys3 = keys.reshape(keys.shape[0], H, DH)
    values3 = values.reshape(values.shape[0], H, DH)
    q_content = (query + head_f[0]).astype(jnp.bfloat16).reshape(row_count, H, DH)
    q_pos = (query + head_f[1]).astype(jnp.bfloat16).reshape(row_count, H, DH)
    q_type = (query + head_f[2]).reshape(row_count, H, DH)
    type_table = head_f[3:5].reshape(2, H, DH)
    type_terms = jnp.einsum("rhe,the->rht", q_type, type_table, precision=HIGHEST_PREC)
    positions = (start + jnp.arange(row_count, dtype=jnp.int32)).astype(jnp.float32)
    q_rel, sin_q, cos_q = relative_queries(q_pos, w_pos, positions)
    query_seg = lax.dynamic_slice_in_dim(seg_row, start, row_count)
    query_kind = lax.dynamic_slice_in_dim(type_row, start, row_count)
    allowed = (query_seg[:, None] == seg_row[None, :])[:, None, :]
    same_type = (query_kind[:, None] == type_row[None, :])[:, None, :]
    scores = score_block(q_content, q_rel, type_terms, keys3, k_rel, same_type)
    masked = jnp.where(allowed, scores, -1e30)
    top = jnp.max(masked, axis=-1, keepdims=True)
    expo = jnp.where(allowed, jnp.exp(masked - top), 0.0)
    total = jnp.sum(expo, axis=-1, keepdims=True)
    probs_b = (expo / total).astype(jnp.bfloat16)
    log_total = top + jnp.log(total)
    attn = (
        jnp.einsum("rhj,jhe->rhe", probs_b, values3, preferred_element_type=jnp.float32)
        .astype(jnp.bfloat16)
        .reshape(row_count, HD)
    )
    branch = jnp.dot(attn, w_out, preferred_element_type=jnp.float32) + biases_f[0]
    first, normed_one, inv_one = layer_norm(
        x_rows.astype(jnp.float32) + branch, gains_f[0], shifts_f[0]
    )
    first_b = first.astype(jnp.bfloat16)
    pre_act = jnp.dot(first_b, w_up, preferred_element_type=jnp.float32) + up_bias.astype(
        jnp.float32
    )
    hidden = gelu_tanh(pre_act).astype(jnp.bfloat16)
    second = jnp.dot(hidden, w_down, preferred_element_type=jnp.float32) + biases_f[1]
    result, normed_two, inv_two = layer_norm(first + second, gains_f[1], shifts_f[1])
    kept = (
        x_rows,
        q_content,
        q_pos,
        q_rel,
        q_type,
        type_terms,
        sin_q,
        cos_q,
        keys3,
        values3,
        allowed,
        same_type,
        log_total,
        attn,
        normed_one,
        inv_one,
        first_b,
        pre_act,
        hidden,
        normed_two,
        inv_two,
    )
    return (result.astype(jnp.bfloat16), kept)


def backward_micro(weights, kept, grad_rows, k_rel, totals):
    w_in, w_out, w_pos, w_up, w_down, head_vec, gains, shifts, biases, up_bias = weights
    (
        x_rows,
        q_content,
        q_pos,
        q_rel,
        q_type,
        type_terms,
        sin_q,
        cos_q,
        keys3,
        values3,
        allowed,
        same_type,
        log_total,
        attn,
        normed_one,
        inv_one,
        first_b,
        pre_act,
        hidden,
        normed_two,
        inv_two,
    ) = kept
    g_in, g_out, g_pos, g_up, g_down, g_head, g_gains, g_shifts, g_bias, g_upbias = totals
    row_count = x_rows.shape[0]
    head_f = head_vec.astype(jnp.float32)
    gains_f = gains.astype(jnp.float32)
    grad_two = grad_rows.astype(jnp.float32)
    gain_two = jnp.sum(grad_two * normed_two, axis=0)
    shift_two = jnp.sum(grad_two, axis=0)
    grad_h2 = norm_back(grad_two, normed_two, inv_two, gains_f[1])
    grad_second = grad_h2.astype(jnp.bfloat16)
    bias_two = jnp.sum(grad_second.astype(jnp.float32), axis=0)
    g_down = g_down + jnp.einsum(
        "rf,rd->fd", hidden, grad_second, preferred_element_type=jnp.float32
    )
    grad_hidden = jnp.einsum("rd,fd->rf", grad_second, w_down, preferred_element_type=jnp.float32)
    act_pull = jax.vjp(gelu_tanh, pre_act)[1]
    grad_pre = act_pull(grad_hidden)[0].astype(jnp.bfloat16)
    g_upbias = g_upbias + jnp.sum(grad_pre.astype(jnp.float32), axis=0)
    g_up = g_up + jnp.einsum("rd,rf->df", first_b, grad_pre, preferred_element_type=jnp.float32)
    grad_first = grad_h2 + jnp.einsum(
        "rf,df->rd", grad_pre, w_up, preferred_element_type=jnp.float32
    )
    gain_one = jnp.sum(grad_first * normed_one, axis=0)
    shift_one = jnp.sum(grad_first, axis=0)
    grad_h1 = norm_back(grad_first, normed_one, inv_one, gains_f[0])
    grad_branch = grad_h1.astype(jnp.bfloat16)
    bias_one = jnp.sum(grad_branch.astype(jnp.float32), axis=0)
    g_out = g_out + jnp.einsum("rk,rd->kd", attn, grad_branch, preferred_element_type=jnp.float32)
    grad_attn = (
        jnp.einsum("rd,kd->rk", grad_branch, w_out, preferred_element_type=jnp.float32)
        .astype(jnp.bfloat16)
        .reshape(row_count, H, DH)
    )
    scores = score_block(q_content, q_rel, type_terms, keys3, k_rel, same_type)
    probs = jnp.where(allowed, jnp.exp(scores - log_total), 0.0)
    grad_probs = jnp.einsum("rhe,jhe->rhj", grad_attn, values3, preferred_element_type=jnp.float32)
    delta = jnp.sum(probs * grad_probs, axis=-1, keepdims=True)
    grad_scores = (probs * (grad_probs - delta)).astype(jnp.bfloat16) * DH ** (-0.5)
    grad_content = jnp.einsum(
        "rhj,jhe->rhe", grad_scores, keys3, preferred_element_type=jnp.float32
    )
    grad_rel = jnp.einsum("rhj,jc->rhc", grad_scores, k_rel, preferred_element_type=jnp.float32)
    probs_b = probs.astype(jnp.bfloat16)
    value_part = jnp.einsum("rhj,rhe->jhe", probs_b, grad_attn, preferred_element_type=jnp.float32)
    key_part = jnp.einsum(
        "rhj,rhe->jhe", grad_scores, q_content, preferred_element_type=jnp.float32
    )
    key_full, value_full = (
        lax.psum_scatter(
            key_part.reshape(key_part.shape[0], HD).astype(jnp.bfloat16),
            "fsdp",
            scatter_dimension=0,
            tiled=True,
        ).astype(jnp.float32),
        lax.psum_scatter(
            value_part.reshape(value_part.shape[0], HD).astype(jnp.bfloat16),
            "fsdp",
            scatter_dimension=0,
            tiled=True,
        ).astype(jnp.float32),
    )
    scores_f = grad_scores.astype(jnp.float32)
    same_f = same_type.astype(jnp.float32)
    grad_same = jnp.sum(scores_f * same_f, axis=-1)
    grad_diff = jnp.sum(scores_f * (1.0 - same_f), axis=-1)
    grad_terms = jnp.stack([grad_diff, grad_same], axis=-1)
    type_table = head_f[3:5].reshape(2, H, DH)
    grad_qtype = jnp.einsum("rht,the->rhe", grad_terms, type_table, precision=HIGHEST_PREC)
    grad_table = jnp.einsum("rht,rhe->the", grad_terms, q_type, precision=HIGHEST_PREC)
    half_width = D // 2
    rel_first = grad_rel[..., :half_width]
    rel_second = grad_rel[..., half_width:]
    grad_proj = jnp.concatenate(
        [rel_first * sin_q - rel_second * cos_q, rel_first * cos_q + rel_second * sin_q], axis=-1
    ).astype(jnp.bfloat16)
    grad_qpos = jnp.einsum(
        "rhc,che->rhe", grad_proj, w_pos.reshape(D, H, DH), preferred_element_type=jnp.float32
    )
    g_pos = g_pos + jnp.einsum(
        "rhc,rhe->che", grad_proj, q_pos, preferred_element_type=jnp.float32
    ).reshape(D, HD)
    head_terms = jnp.stack(
        [
            jnp.sum(grad_content.reshape(row_count, HD), axis=0),
            jnp.sum(grad_qpos.reshape(row_count, HD), axis=0),
            jnp.sum(grad_qtype.reshape(row_count, HD), axis=0),
            grad_table[0].reshape(HD),
            grad_table[1].reshape(HD),
        ]
    )
    g_head = g_head + head_terms
    grad_query = (grad_content + grad_qpos + grad_qtype).reshape(row_count, HD).astype(jnp.bfloat16)
    grad_proj_in = jnp.concatenate(
        [grad_query, key_full.astype(jnp.bfloat16), value_full.astype(jnp.bfloat16)], axis=1
    )
    g_in = g_in + jnp.einsum("rd,rk->dk", x_rows, grad_proj_in, preferred_element_type=jnp.float32)
    grad_x = grad_h1 + jnp.einsum(
        "rk,dk->rd", grad_proj_in, w_in, preferred_element_type=jnp.float32
    )
    g_gains = g_gains + jnp.stack([gain_one, gain_two])
    g_shifts = g_shifts + jnp.stack([shift_one, shift_two])
    g_bias = g_bias + jnp.stack([bias_one, bias_two])
    return (grad_x, (g_in, g_out, g_pos, g_up, g_down, g_head, g_gains, g_shifts, g_bias, g_upbias))


def per_device(
    tokens,
    seg_ids,
    token_types,
    attn_in,
    attn_out,
    pos_kernel,
    ffn_in,
    ffn_out,
    head_vectors,
    norm_gains,
    norm_shifts,
    out_bias,
    ffn_bias,
    cotangent,
):
    shards = (
        attn_in,
        attn_out,
        pos_kernel,
        ffn_in,
        ffn_out,
        head_vectors,
        norm_gains,
        norm_shifts,
        out_bias,
        ffn_bias,
    )
    micro_count = tokens.shape[0]
    row_count = tokens.shape[1]
    start = lax.axis_index("fsdp") * row_count
    all_positions = jnp.arange(seg_ids.shape[1], dtype=jnp.float32)
    key_sin, key_cos = angle_tables(all_positions, D)
    k_rel = jnp.concatenate([key_cos, key_sin], axis=-1).astype(jnp.bfloat16)
    totals = (
        jnp.zeros((D, 3 * HD), jnp.float32),
        jnp.zeros((HD, D), jnp.float32),
        jnp.zeros((D, HD), jnp.float32),
        jnp.zeros((D, FF), jnp.float32),
        jnp.zeros((FF, D), jnp.float32),
        jnp.zeros((5, HD), jnp.float32),
        jnp.zeros((2, D), jnp.float32),
        jnp.zeros((2, D), jnp.float32),
        jnp.zeros((2, D), jnp.float32),
        jnp.zeros((FF,), jnp.float32),
    )
    results = []
    input_grads = []
    for micro_step in range(micro_count):
        forward_weights = fetch_forward(shards)
        result, kept = forward_micro(
            forward_weights,
            tokens[micro_step],
            seg_ids[micro_step],
            token_types[micro_step],
            start,
            k_rel,
        )
        backward_weights = fetch_backward(shards)
        grad_x, totals = backward_micro(
            backward_weights, kept, cotangent[micro_step], k_rel, totals
        )
        results.append(result)
        input_grads.append(grad_x)
    final = (
        lax.psum_scatter(totals[0], ("dp", "fsdp"), scatter_dimension=0, tiled=True),
        lax.psum_scatter(totals[1], ("dp", "fsdp"), scatter_dimension=0, tiled=True),
        lax.psum_scatter(totals[2], ("dp", "fsdp"), scatter_dimension=0, tiled=True),
        lax.psum_scatter(totals[3], ("dp", "fsdp"), scatter_dimension=0, tiled=True),
        lax.psum_scatter(totals[4], ("dp", "fsdp"), scatter_dimension=0, tiled=True),
        lax.psum_scatter(totals[5], ("dp", "fsdp"), scatter_dimension=1, tiled=True),
        lax.psum_scatter(totals[6], ("dp", "fsdp"), scatter_dimension=1, tiled=True),
        lax.psum_scatter(totals[7], ("dp", "fsdp"), scatter_dimension=1, tiled=True),
        lax.psum_scatter(totals[8], ("dp", "fsdp"), scatter_dimension=1, tiled=True),
        lax.psum_scatter(totals[9], ("dp", "fsdp"), scatter_dimension=0, tiled=True),
    )
    return (
        jnp.stack(results),
        jnp.stack(input_grads),
        final[0],
        final[1],
        final[2],
        final[3],
        final[4],
        final[5],
        final[6],
        final[7],
        final[8],
        final[9],
    )


def solution(mesh):
    placed = (
        P("dp", "fsdp", None),
        P("dp", None),
        P("dp", None),
        P(("dp", "fsdp"), None),
        P(("dp", "fsdp"), None),
        P(("dp", "fsdp"), None),
        P(("dp", "fsdp"), None),
        P(("dp", "fsdp"), None),
        P(None, ("dp", "fsdp")),
        P(None, ("dp", "fsdp")),
        P(None, ("dp", "fsdp")),
        P(None, ("dp", "fsdp")),
        P(("dp", "fsdp")),
        P("dp", "fsdp", None),
    )
    return jax.shard_map(
        per_device,
        mesh=mesh,
        in_specs=placed,
        out_specs=(
            P("dp", "fsdp", None),
            P("dp", "fsdp", None),
            P(("dp", "fsdp"), None),
            P(("dp", "fsdp"), None),
            P(("dp", "fsdp"), None),
            P(("dp", "fsdp"), None),
            P(("dp", "fsdp"), None),
            P(None, ("dp", "fsdp")),
            P(None, ("dp", "fsdp")),
            P(None, ("dp", "fsdp")),
            P(None, ("dp", "fsdp")),
            P(("dp", "fsdp")),
        ),
        check_vma=False,
    )
```

profile of v0, /device:TPU:0, one launch (start us, length us, event | category | flops | bytes accessed | tf_op | source)
XLA Modules:
  0.0 1424.0 jit_solution(12708316016578102482)
XLA Ops:
  8.7 65.0 %all-gather.14.cloned.1.call-done = bf16[768,2304]{1,0:T(8,128)(2,1)} async-done(((bf16[24,2304]{1,0:T(8,128)(2,1)}), bf16[768,2304]{1,0:T(8,128)(2,1)}) %all-gather.14.cloned.1.call-update) | async-done | bytes 3538960 | tf_op jit(solution)/shard_map/all_gather | solution.py:51
  73.7 4.0 fusion.175
  84.7 66.2 %all-gather.1 = bf16[32,24,2]{1,2,0:T(2,128)(2,1)S(1)} all-gather(bf16[1,24,2]{1,2,0:T(2,128)(2,1)S(1)} %bitcast.356), channel_id=1, replica_groups=mesh['dp'=4,'fsdp'=8] {'dp','fsdp'}, dimensions={0}, use_global_device_ids=true | all-gather | bytes 3168 | tf_op jit(solution)/shard_map/all_gather | solution.py:59
  152.1 37.9 %all-reduce = bf16[3072]{0:T(1024)(128)(2,1)S(1)} all-reduce(bf16[3072]{0:T(1024)(128)(2,1)S(1)} %dynamic-update-slice), channel_id=1, replica_groups=mesh['dp'=4,'fsdp'=8] {'dp','fsdp'}, use_global_device_ids=true, to_apply=%add | all-reduce | flops 3072 | bytes 12288
  190.5 66.3 %all-gather = bf16[32,24,5]{1,2,0:T(8,128)(2,1)S(1)} all-gather(bf16[1,24,5]{1,2,0:T(8,128)(2,1)S(1)} %bitcast.355), channel_id=1, replica_groups=mesh['dp'=4,'fsdp'=8] {'dp','fsdp'}, dimensions={0}, use_global_device_ids=true | all-gather | bytes 7920 | tf_op jit(solution)/shard_map/all_gather | solution.py:56
  257.0 64.1 %all-gather.3 = bf16[32,24,2]{1,2,0:T(2,128)(2,1)S(1)} all-gather(bf16[1,24,2]{1,2,0:T(2,128)(2,1)} %bitcast.357), channel_id=1, replica_groups=mesh['dp'=4,'fsdp'=8] {'dp','fsdp'}, dimensions={0}, use_global_device_ids=true | all-gather | bytes 3168 | tf_op jit(solution)/shard_map/all_gather | solution.py:58
  321.4 65.9 %all-gather.2 = bf16[32,24,2]{1,2,0:T(2,128)(2,1)S(1)} all-gather(bf16[1,24,2]{1,2,0:T(2,128)(2,1)} %bitcast.358), channel_id=1, replica_groups=mesh['dp'=4,'fsdp'=8] {'dp','fsdp'}, dimensions={0}, use_global_device_ids=true | all-gather | bytes 3168 | tf_op jit(solution)/shard_map/all_gather | solution.py:57
  395.1 6.0 cosine_convert_fusion
  416.3 3.9 convolution_bitcast_fusion.1
  420.3 3.0 convolution_bitcast_fusion
  424.5 4.5 add_convert_fusion.3
  429.0 4.5 fusion.32
  433.5 4.5 fusion.36
  439.9 5.6 select_reduce_fusion.1
  451.3 5.4 fusion.72
  461.0 3.8 convolution_add_fusion.3
  464.9 4.1 fusion.177
  469.8 5.1 select_reduce_fusion
  478.2 18.4 %all-gather.28.cloned.1.call-done = bf16[1024,768]{1,0:T(8,128)(2,1)} async-done(((bf16[128,768]{1,0:T(8,128)(2,1)}), bf16[1024,768]{1,0:T(8,128)(2,1)}) %all-gather.28.cloned.1.call-update) | async-done | bytes 1572880 | tf_op jit(solution)/shard_map/all_gather | solution.py:115
  496.6 2.8 copy.151
  499.4 5.4 fusion.71
  506.7 4.6 fusion.180
  514.3 2.9 convert_reduce_fusion.1
  519.6 2.9 convert_reduce_fusion
  522.5 3.1 convert_reduce_fusion.7
  527.4 4.1 fusion.43
  534.2 12.0 fusion.4
  546.2 3.3 convolution_convert_fusion
  552.1 2.7 convolution_convert_fusion.3
  557.3 5.3 fusion.40
  566.9 13.2 fusion.2
  580.1 4.4 convolution_convert_fusion.1
  591.1 5.1 fusion.157
  596.3 2.7 fusion.156
  604.8 3.1 copy.171
  610.9 3.0 fusion.64
  621.5 43.9 %reduce-scatter.36.cloned.1.call-done = bf16[128,768]{1,0:T(8,128)(2,1)} async-done(((bf16[1024,768]{1,0:T(8,128)(2,1)}), bf16[128,768]{1,0:T(8,128)(2,1)}) %reduce-scatter.36.cloned.1.call-update) | async-done | bytes 196624
  666.5 66.5 %reduce-scatter.34.cloned.1.call-done = bf16[128,768]{1,0:T(8,128)(2,1)} async-done(((bf16[1024,768]{1,0:T(8,128)(2,1)}), bf16[128,768]{1,0:T(8,128)(2,1)}) %reduce-scatter.34.cloned.1.call-update) | async-done | bytes 196624
  734.1 66.7 %reduce-scatter.32.cloned.1.call-done = bf16[128,768]{1,0:T(8,128)(2,1)} async-done(((bf16[1024,768]{1,0:T(8,128)(2,1)}), bf16[128,768]{1,0:T(8,128)(2,1)}) %reduce-scatter.32.cloned.1.call-update) | async-done | bytes 196624
  803.0 4.0 add_bitcast_fusion
  807.0 8.1 copy.193
  817.7 5.2 convolution_add_fusion.1
  826.9 5.4 convolution_add_fusion
  871.3 41.7 %all-reduce.6 = (f32[5,768]{1,0:T(8,128)}, f32[2,768]{1,0:T(2,128)}, f32[2,768]{1,0:T(2,128)}, f32[2,768]{1,0:T(2,128)}, f32[3072]{0:T(1024)}) all-reduce(f32[5,768]{1,0:T(8,128)} %add.413, f32[2,768]{1,0:T(2,128)} %maximum_add_fusion, f32[2,768]{1,0:T(2,128)} %maximum_add_fusion.1, ...), channel_id=11, replica_groups=mesh['dp'=4,'fsdp'=8] {'dp','fsdp'}, use_global_device_ids=true, to_apply=%region_41.42.clone | all-reduce | flops 11520 | bytes 92160
  926.4 82.9 %reduce-scatter.26.cloned.1.call-done = f32[24,768]{1,0:T(8,128)} async-done(((f32[768,768]{1,0:T(8,128)}), f32[24,768]{1,0:T(8,128)}) %reduce-scatter.26.cloned.1.call-update) | async-done | bytes 73744 | tf_op jit(solution)/shard_map/reduce_scatter | solution.py:375
  1009.3 124.7 %reduce-scatter.40.cloned.1.call-done = f32[24,2304]{1,0:T(8,128)} async-done(((f32[768,2304]{1,0:T(8,128)}), f32[24,2304]{1,0:T(8,128)}) %reduce-scatter.40.cloned.1.call-update) | async-done | bytes 221200
  1134.0 141.4 %reduce-scatter.28.cloned.1.call-done = f32[24,3072]{1,0:T(8,128)} async-done(((f32[768,3072]{1,0:T(8,128)}), f32[24,3072]{1,0:T(8,128)}) %reduce-scatter.28.cloned.1.call-update) | async-done | bytes 294928 | tf_op jit(solution)/shard_map/reduce_scatter | solution.py:376
  1275.5 141.5 %reduce-scatter.30.cloned.1.call-done = f32[96,768]{1,0:T(8,128)} async-done(((f32[3072,768]{1,0:T(8,128)}), f32[96,768]{1,0:T(8,128)}) %reduce-scatter.30.cloned.1.call-update) | async-done | bytes 294928 | tf_op jit(solution)/shard_map/reduce_scatter | solution.py:377
  (452 shorter events, 157.0 us)
Async XLA Ops:
  7.2 66.5 %all-gather.14.cloned.1.call-start = ((), (), s32[]{:S(2)}) async-start(), calls=%async_computation.9 | async-start | bytes 3649536 | tf_op jit(solution)/shard_map/all_gather | solution.py:51
  7.9 393.3 %all-gather.20.cloned.1.call-start = ((), (), s32[]{:S(2)}) async-start(), calls=%async_computation.12 | async-start | bytes 1216512 | tf_op jit(solution)/shard_map/all_gather | solution.py:53
  8.7 429.4 %all-gather.18.cloned.1.call-start = ((), (), s32[]{:S(2)}) async-start(), calls=%async_computation.11 | async-start | bytes 1769472 | tf_op jit(solution)/shard_map/all_gather | solution.py:114
  78.4 371.0 %all-gather.16.cloned.1.call-start = ((), (), s32[]{:S(2)}) async-start(), calls=%async_computation.10 | async-start | bytes 1769472 | tf_op jit(solution)/shard_map/all_gather | solution.py:115
  79.0 377.7 %all-gather.22.cloned.1.call-start = ((), (), s32[]{:S(2)}) async-start(), calls=%async_computation.13 | async-start | bytes 1216512 | tf_op jit(solution)/shard_map/all_gather | solution.py:52
  79.6 110.9 %copy-start.115 = (bf16[5,24]{1,0:T(8,128)(2,1)S(1)}, bf16[5,24]{1,0:T(8,128)(2,1)}, u32[]{:S(2)}) copy-start(bf16[5,24]{1,0:T(8,128)(2,1)} %param.22) | copy-start | bytes 724
  79.6 308.0 %copy-start.110 = (s32[2,1024]{1,0:T(2,128)S(1)}, s32[2,1024]{1,0:T(2,128)}, u32[]{:S(2)}) copy-start(s32[2,1024]{1,0:T(2,128)} %param.15) | copy-start | bytes 24580
  79.6 379.6 %all-gather.30.cloned.1.call-start = ((), (), s32[]{:S(2)}) async-start(), calls=%async_computation.17 | async-start | bytes 1769472 | tf_op jit(solution)/shard_map/all_gather | solution.py:114
  83.1 377.9 %all-gather.24.cloned.1.call-start = ((), (), s32[]{:S(2)}) async-start(), calls=%async_computation.14 | async-start | bytes 4866048 | tf_op jit(solution)/shard_map/all_gather | solution.py:54
  83.9 381.0 %all-gather.26.cloned.1.call-start = ((), (), s32[]{:S(2)}) async-start(), calls=%async_computation.15 | async-start | bytes 4866048 | tf_op jit(solution)/shard_map/all_gather | solution.py:55
  84.6 411.9 %all-gather.28.cloned.1.call-start = ((), (), s32[]{:S(2)}) async-start(), calls=%async_computation.16 | async-start | bytes 1769472 | tf_op jit(solution)/shard_map/all_gather | solution.py:115
  388.4 12.8 copy-start.88
  388.4 12.8 copy-start.89
  388.4 14.8 %copy-start.116 = (s32[128]{0:T(128)}, s32[128]{0:T(128)S(1)}, u32[]{:S(2)}) copy-start(s32[128]{0:T(128)S(1)} %fusion.111) | copy-start | bytes 1540
  388.5 14.8 %copy-start.117 = (s32[128]{0:T(128)}, s32[128]{0:T(128)S(1)}, u32[]{:S(2)}) copy-start(s32[128]{0:T(128)S(1)} %fusion.113) | copy-start | bytes 1540
  401.2 32.3 %copy-start.16 = (bf16[1024,384]{1,0:T(8,128)(2,1)}, bf16[1024,384]{1,0:T(8,128)(2,1)S(1)}, u32[]{:S(2)}) copy-start(bf16[1024,384]{1,0:T(8,128)(2,1)S(1)} %get-tuple-element.164) | copy-start | bytes 2359300
  401.2 32.3 %copy-start.18 = (bf16[1024,384]{1,0:T(8,128)(2,1)}, bf16[1024,384]{1,0:T(8,128)(2,1)S(1)}, u32[]{:S(2)}) copy-start(bf16[1024,384]{1,0:T(8,128)(2,1)S(1)} %get-tuple-element.165) | copy-start | bytes 2359300
  403.3 16.9 %copy-start.12 = (bf16[768,768]{0,1:T(8,128)(2,1)}, bf16[768,768]{0,1:T(8,128)(2,1)S(1)}, u32[]{:S(2)}) copy-start(bf16[768,768]{0,1:T(8,128)(2,1)S(1)} %copy.140) | copy-start | bytes 3538948
  406.1 14.2 copy-start.38
  423.3 197.0 %reduce-scatter.38.cloned.1.call-start = ((), (), s32[]{:S(2)}) async-start(), calls=%async_computation.25 | async-start | bytes 1769472
  461.0 8.8 copy-start.10
  464.8 49.4 %copy-start.14 = (f32[128,3072]{1,0:T(8,128)}, f32[128,3072]{1,0:T(8,128)S(1)}, u32[]{:S(2)}) copy-start(f32[128,3072]{1,0:T(8,128)S(1)} %convolution_add_fusion.3) | copy-start | bytes 4718596
  477.6 21.8 %copy-start.48 = (pred[128,1024]{0,1:T(8,128)(4,1)S(1)}, pred[128,1024]{0,1:T(8,128)(4,1)}, u32[]{:S(2)}) copy-start(pred[128,1024]{0,1:T(8,128)(4,1)} %broadcast_compare_fusion.1) | copy-start | bytes 393220
  478.2 21.2 %copy-start.78 = (f32[128,12]{0,1:T(8,128)S(1)}, f32[128,12]{0,1:T(8,128)}, u32[]{:S(2)}) copy-start(f32[128,12]{0,1:T(8,128)} %copy-done.77) | copy-start | bytes 18436
  496.6 9.1 slice-start
  505.4 20.2 %copy-start.6 = (f32[128,768]{1,0:T(8,128)}, f32[128,768]{1,0:T(8,128)S(1)}, u32[]{:S(2)}) copy-start(f32[128,768]{1,0:T(8,128)S(1)} %get-tuple-element.179) | copy-start | bytes 1179652
  505.4 20.2 %copy-start.104 = (f32[128]{0:T(128)}, f32[128]{0:T(128)S(1)}, u32[]{:S(2)}) copy-start(f32[128]{0:T(128)S(1)} %broadcast_multiply_fusion.9) | copy-start | bytes 1540
  505.7 20.0 %copy-start.108 = (f32[128]{0:T(128)}, f32[128]{0:T(128)S(1)}, u32[]{:S(2)}) copy-start(f32[128]{0:T(128)S(1)} %add_rsqrt_fusion.1) | copy-start | bytes 1540
  505.7 8.5 slice-start.2
  506.6 13.0 copy-start.21
  533.1 132.3 %reduce-scatter.36.cloned.1.call-start = ((), (), s32[]{:S(2)}) async-start(), calls=%async_computation.24 | async-start | bytes 1769472
  552.1 180.9 %reduce-scatter.34.cloned.1.call-start = ((), (), s32[]{:S(2)}) async-start(), calls=%async_computation.23 | async-start | bytes 1769472
  565.2 235.6 %reduce-scatter.32.cloned.1.call-start = ((), (), s32[]{:S(2)}) async-start(), calls=%async_computation.22 | async-start | bytes 1769472
  587.1 339.3 %reduce-scatter.24.cloned.1.call-start = ((), (), s32[]{:S(2)}) async-start(), calls=%async_computation.18 | async-start | bytes 2433024 | tf_op jit(solution)/shard_map/reduce_scatter | solution.py:374
  591.1 418.2 %reduce-scatter.26.cloned.1.call-start = ((), (), s32[]{:S(2)}) async-start(), calls=%async_computation.19 | async-start | bytes 2433024 | tf_op jit(solution)/shard_map/reduce_scatter | solution.py:375
  607.9 526.1 %reduce-scatter.40.cloned.1.call-start = ((), (), s32[]{:S(2)}) async-start(), calls=%async_computation.26 | async-start | bytes 7299072
  610.2 8.9 copy-start.83
  616.0 187.0 %copy-start.58 = (bf16[128,12,64]{0,2,1:T(8,128)(2,1)}, bf16[128,12,64]{0,2,1:T(8,128)(2,1)S(1)}, u32[]{:S(2)}) copy-start(bf16[128,12,64]{0,2,1:T(8,128)(2,1)S(1)} %get-tuple-element.132) | copy-start | bytes 589828
  619.1 182.7 %copy-start.33 = (bf16[2,128,768]{2,1,0:T(8,128)(2,1)S(1)}, bf16[2,128,768]{2,1,0:T(8,128)(2,1)}, u32[]{:S(2)}) copy-start(bf16[2,128,768]{2,1,0:T(8,128)(2,1)} %param.14) | copy-start | bytes 1179652
  620.4 182.6 %copy-start.66 = (bf16[128,12,64]{0,2,1:T(8,128)(2,1)}, bf16[128,12,64]{0,2,1:T(8,128)(2,1)S(1)}, u32[]{:S(2)}) copy-start(bf16[128,12,64]{0,2,1:T(8,128)(2,1)S(1)} %get-tuple-element.136) | copy-start | bytes 589828
  621.5 181.4 %copy-start.56 = (bf16[128,768]{0,1:T(8,128)(2,1)}, bf16[128,768]{0,1:T(8,128)(2,1)S(1)}, u32[]{:S(2)}) copy-start(bf16[128,768]{0,1:T(8,128)(2,1)S(1)} %copy.192) | copy-start | bytes 589828
  666.5 136.5 %copy-start.57 = (bf16[128,768]{0,1:T(8,128)(2,1)}, bf16[128,768]{0,1:T(8,128)(2,1)S(1)}, u32[]{:S(2)}) copy-start(bf16[128,768]{0,1:T(8,128)(2,1)S(1)} %copy.190) | copy-start | bytes 589828
  734.1 68.8 %copy-start.62 = (bf16[128,768]{0,1:T(8,128)(2,1)}, bf16[128,768]{0,1:T(8,128)(2,1)S(1)}, u32[]{:S(2)}) copy-start(bf16[128,768]{0,1:T(8,128)(2,1)S(1)} %copy.188) | copy-start | bytes 589828
  815.1 460.3 %reduce-scatter.28.cloned.1.call-start = ((), (), s32[]{:S(2)}) async-start(), calls=%async_computation.20 | async-start | bytes 9732096 | tf_op jit(solution)/shard_map/reduce_scatter | solution.py:376
  822.9 594.0 %reduce-scatter.30.cloned.1.call-start = ((), (), s32[]{:S(2)}) async-start(), calls=%async_computation.21 | async-start | bytes 9732096 | tf_op jit(solution)/shard_map/reduce_scatter | solution.py:377
  832.3 15.8 %copy-start.80 = (f32[128,12,1]{0,2,1:T(1,128)S(1)}, f32[128,12,1]{0,2,1:T(1,128)}, u32[]{:S(2)}) copy-start(f32[128,12,1]{0,2,1:T(1,128)} %copy-done.79) | copy-start | bytes 18436
  832.3 15.8 %copy-start.82 = (f32[128,12,1]{0,2,1:T(1,128)S(1)}, f32[128,12,1]{0,2,1:T(1,128)}, u32[]{:S(2)}) copy-start(f32[128,12,1]{0,2,1:T(1,128)} %copy-done.81) | copy-start | bytes 18436
  832.3 89.1 %copy-start.3 = (bf16[768,2304]{1,0:T(8,128)(2,1)S(1)}, bf16[768,2304]{1,0:T(8,128)(2,1)}, u32[]{:S(2)}) copy-start(bf16[768,2304]{1,0:T(8,128)(2,1)} %all-gather.14.cloned.1.call-done) | copy-start | bytes 10616836
  (94 other events, 321.0 us)
Sparse Core Ops, SparseCore 0:
  10.9 62.7 all-gather.13
  76.6 52.8 all-gather.19
  132.2 43.7 all-gather.17
  178.7 42.7 all-gather.15
  224.2 52.4 all-gather.21
  278.7 43.1 all-gather.29
  324.9 62.0 all-gather.23
  389.9 61.9 all-gather.25
  454.0 42.5 all-gather.27
  533.3 64.0 reduce-scatter.37
  600.8 64.5 reduce-scatter.35
  668.7 64.2 reduce-scatter.33
  736.4 64.2 reduce-scatter.31
  806.5 98.4 reduce-scatter.23
  910.7 98.5 reduce-scatter.25
  1015.4 118.5 reduce-scatter.39
  1140.3 135.0 reduce-scatter.27
  1281.8 135.1 reduce-scatter.29
where the time goes:
time: 1430 us; the launch traced here: 1420 us
  waiting for transfers between devices  755 us (53%)
  blocking collectives  342 us (24%)
  matrix products  165 us (12%)
  local copies, waits for them, and re-layouts  101 us (7%)
  other arithmetic  42.4 us (3%)
  between operations  16.4 us (1%)
    unnamed x23, waiting for transfers between devices  306 us
    reduce_scatter x1, waiting for transfers between devices, per_device(): lax.psum_scatter(totals[4], ('dp', 'fsdp'), scatter_dimension=0, tiled=True)  142 us
    reduce_scatter x1, waiting for transfers between devices, per_device(): lax.psum_scatter(totals[3], ('dp', 'fsdp'), scatter_dimension=0, tiled=True)  141 us
    reduce_scatter x1, waiting for transfers between devices, per_device(): lax.psum_scatter(totals[2], ('dp', 'fsdp'), scatter_dimension=0, tiled=True)  82.9 us
    unnamed x2, blocking collectives  79.6 us
    all_gather x1, blocking collectives, fetch_forward(): lax.all_gather(shards[5], ('dp', 'fsdp'), axis=1, tiled=True)  66.3 us
    all_gather x1, blocking collectives, fetch_forward(): lax.all_gather(shards[8], ('dp', 'fsdp'), axis=1, tiled=True)  66.2 us
    all_gather x1, blocking collectives, fetch_forward(): lax.all_gather(shards[6], ('dp', 'fsdp'), axis=1, tiled=True)  65.9 us
  transfers between devices with their start and end apart: 18, of which 9 were waited for; matrix products, arithmetic and copies ran while one was open for 18% of the time, Pallas kernels for 0%

commit v1 on v0

--- a/solution.py
+++ b/solution.py
@@ -1,6 +1,11 @@
+import functools
+
 import jax
 import jax.numpy as jnp
+import numpy as np
 from jax import lax
+from jax.experimental import pallas as pl
+from jax.experimental.pallas import tpu as pltpu
 from jax.sharding import PartitionSpec as P
 
 D = 768
@@ -397,6 +402,1006 @@
     )
 
 
+MESH_ID = pl.DeviceIdType.MESH
+Z_OFFSETS = (0, -1, 1, -2, 2, -3, 3)
+ANY_SPEC = pl.BlockSpec(memory_space=pl.ANY)
+VMEM_SPEC = pl.BlockSpec(memory_space=pltpu.VMEM)
+
+
+def place():
+    dp = lax.axis_index("dp")
+    fs = lax.axis_index("fsdp")
+    return (dp // 2, dp % 2, fs // 2, fs % 2)
+
+
+def device(x, c, z, y):
+    return (x * 2 + c, z * 2 + y)
+
+
+def guarded(cond, action):
+    if cond is None:
+        action()
+    else:
+        pl.when(cond)(action)
+
+
+def greet(peers):
+    barrier = pltpu.get_barrier_semaphore()
+    for cond, peer in peers:
+        guarded(
+            cond,
+            lambda peer=peer: pl.semaphore_signal(
+                barrier, inc=1, device_id=peer, device_id_type=MESH_ID
+            ),
+        )
+    count = 0
+    for cond, _ in peers:
+        count = count + (1 if cond is None else cond.astype(jnp.int32))
+    pl.semaphore_wait(barrier, count)
+
+
+def remote(src, dst, send, recv, to):
+    return pltpu.make_async_remote_copy(
+        src_ref=src, dst_ref=dst, send_sem=send, recv_sem=recv, device_id=to, device_id_type=MESH_ID
+    )
+
+
+def half_members(kinds, half):
+    if half == 0:
+        return range(len(kinds))
+    return [a for a, kind in enumerate(kinds) if kind in ("split", half)]
+
+
+def swap_peers():
+    x, c, z, y = place()
+    peers = []
+    for m in range(2):
+        away = jnp.logical_or(z // 2 != c, z % 2 != m)
+        peers.append((away, device(x, z // 2, 2 * c + m, y)))
+    return peers
+
+
+def swap_copies(src, dst, send, recv, local):
+    x, c, z, y = place()
+
+    def both(m):
+        peer = device(x, z // 2, 2 * c + m, y)
+        out = remote(src.at[m], dst.at[z % 2], send.at[m], recv.at[z % 2], peer)
+        into = remote(src.at[m], dst.at[m], send.at[m], recv.at[m], peer)
+        here = pltpu.make_async_copy(src.at[m], dst.at[m], local.at[m])
+        away = jnp.logical_or(z // 2 != c, z % 2 != m)
+        return (out, into, here, away)
+
+    def start():
+        for m in range(2):
+            out, _, here, away = both(m)
+            pl.when(away)(out.start)
+            pl.when(jnp.logical_not(away))(here.start)
+
+    def wait():
+        for m in range(2):
+            out, into, here, away = both(m)
+            pl.when(away)(into.wait_recv)
+            pl.when(away)(out.wait_send)
+            pl.when(jnp.logical_not(away))(here.wait)
+
+    return (start, wait)
+
+
+def gather_kernel(kinds, swaps, pairs, *refs):
+    n = len(kinds)
+    srcs, refs = (refs[:n], refs[n:])
+    swap_in, refs = (refs[:swaps], refs[swaps:])
+    pair_in, refs = (refs[:pairs], refs[pairs:])
+    dsts, refs = (refs[:n], refs[n:])
+    swap_out, refs = (refs[:swaps], refs[swaps:])
+    pair_out, refs = (refs[:pairs], refs[pairs:])
+    send_sem, recv_sem, local_sem, swap_sem, pair_sem = refs
+    x, c, z, y = place()
+    below, above = (z > 0, z < 3)
+    nx, ny, partner = (device(1 - x, c, z, y), device(x, c, z, 1 - y), device(x, 1 - c, z, y))
+    up, down = (
+        device(x, c, jnp.minimum(z + 1, 3), y),
+        device(x, c, jnp.maximum(z - 1, 0), y),
+    )
+    peers = [(None, nx), (None, ny), (None, partner), (below, down), (above, up)]
+    if swaps:
+        peers += swap_peers()
+    greet(peers)
+
+    def slot(a, core, xx, yy, k, half):
+        i = (xx * 2 + core) * 8 + k * 2 + yy
+        if kinds[a] == "split":
+            if half == 0:
+                return dsts[a].at[:, i]
+            return dsts[a].at[0:2, i] if half == 1 else dsts[a].at[2:4, i]
+        return dsts[a].at[i]
+
+    def copies(kind, k, owner, half, to, core, own=False):
+        out = []
+        for a in half_members(kinds, half):
+            there = slot(a, core, owner[0], owner[1], k, half)
+            out.append(
+                remote(
+                    srcs[a] if own else there,
+                    there,
+                    send_sem.at[kind, a, k],
+                    recv_sem.at[kind, a, k],
+                    to,
+                )
+            )
+        return out
+
+    started = []
+
+    def send(cond, kind, k, owner, half, to, own=False):
+        def go():
+            for copy in copies(kind, k, owner, half, to, c, own):
+                copy.start()
+
+        def finish():
+            for copy in copies(kind, k, owner, half, to, c, own):
+                copy.wait_send()
+
+        guarded(cond, go)
+        started.append((cond, finish))
+
+    def recv(cond, kind, k, owner, half, core):
+        def go():
+            for copy in copies(kind, k, owner, half, partner, core):
+                copy.wait_recv()
+
+        guarded(cond, go)
+
+    k_up, k_down, k_x, k_y, k_h1, k_h2, p_own, p_x, p_y, p_opp = range(10)
+    me, at_x, at_y, opposite = ((x, y), (1 - x, y), (x, 1 - y), (1 - x, 1 - y))
+
+    def level(off):
+        k = z + off
+        if off == 0:
+            return (k, None)
+        return (jnp.clip(k, 0, 3), k >= 0 if off < 0 else k <= 3)
+
+    def both(cond, other):
+        return other if cond is None else jnp.logical_and(cond, other)
+
+    def column(off):
+        k, ok = level(off)
+        own = off == 0
+        if off < 0:
+            recv(ok, k_up, k, me, 0, c)
+        if off > 0:
+            recv(ok, k_down, k, me, 0, c)
+        if off <= 0:
+            send(both(ok, above), k_up, k, me, 0, up, own)
+        if off >= 0:
+            send(both(ok, below), k_down, k, me, 0, down, own)
+        send(ok, k_x, k, me, 0, nx, own)
+        send(ok, k_y, k, me, 0, ny, own)
+        send(ok, p_own, k, me, 0, partner, own)
+
+    def beside(off):
+        k, ok = level(off)
+        recv(ok, k_x, k, at_x, 0, c)
+        send(ok, k_h1, k, at_x, 1, ny)
+        send(ok, p_x, k, at_x, 0, partner)
+        recv(ok, k_y, k, at_y, 0, c)
+        send(ok, k_h2, k, at_y, 2, nx)
+        send(ok, p_y, k, at_y, 0, partner)
+
+    def across(off):
+        k, ok = level(off)
+        recv(ok, k_h1, k, opposite, 1, c)
+        recv(ok, k_h2, k, opposite, 2, c)
+        send(ok, p_opp, k, opposite, 0, partner)
+
+    locals_ = []
+    for a in range(n):
+        copy = pltpu.make_async_copy(srcs[a], slot(a, c, x, y, z, 0), local_sem.at[a])
+        copy.start()
+        locals_.append(copy)
+    for act, off in (
+        (column, 0),
+        ("pairs", 0),
+        (column, -1),
+        (column, 1),
+        (beside, 0),
+        (column, -2),
+        (column, 2),
+        (beside, -1),
+        (beside, 1),
+        (across, 0),
+        (column, -3),
+        (column, 3),
+        ("swaps", 0),
+        (beside, -2),
+        (beside, 2),
+        (across, -1),
+        (across, 1),
+        (beside, -3),
+        (beside, 3),
+        (across, -2),
+        (across, 2),
+        (across, -3),
+        (across, 3),
+    ):
+        if act == "swaps":
+            moves = [
+                swap_copies(
+                    swap_in[i], swap_out[i], swap_sem.at[i, 0], swap_sem.at[i, 1], swap_sem.at[i, 2]
+                )
+                for i in range(swaps)
+            ]
+            for start, _ in moves:
+                start()
+        elif act == "pairs":
+            for i in range(pairs):
+                row = pair_in[i].at[z % 2]
+
+                @pl.when(c == z // 2)
+                def _(row=row, i=i):
+                    remote(row, pair_out[i], pair_sem.at[i, 0], pair_sem.at[i, 1], partner).start()
+                    pltpu.make_async_copy(row, pair_out[i], pair_sem.at[i, 2]).start()
+        else:
+            act(off)
+    for k in range(4):
+        for kind, owner in ((p_own, me), (p_x, at_x), (p_y, at_y), (p_opp, opposite)):
+            recv(None, kind, k, owner, 0, 1 - c)
+    for cond, finish in started:
+        guarded(cond, finish)
+    for copy in locals_:
+        copy.wait()
+    for _, wait in moves:
+        wait()
+    for i in range(pairs):
+        row = pair_in[i].at[z % 2]
+        over = remote(row, pair_out[i], pair_sem.at[i, 0], pair_sem.at[i, 1], partner)
+        here = pltpu.make_async_copy(row, pair_out[i], pair_sem.at[i, 2])
+
+        @pl.when(c == z // 2)
+        def _(over=over, here=here):
+            over.wait_send()
+            here.wait()
+
+        pl.when(c != z // 2)(over.wait_recv)
+
+
+def gather(kinds, arrays, swaps, pairs, collective_id):
+    n, s, p = (len(arrays), len(swaps), len(pairs))
+    outs = []
+    for kind, array in zip(kinds, arrays):
+        shape = array.shape[:1] + (32,) + array.shape[1:] if kind == "split" else (32,) + array.shape
+        outs.append(jax.ShapeDtypeStruct(shape, array.dtype))
+    outs += [jax.ShapeDtypeStruct(a.shape, a.dtype) for a in swaps]
+    outs += [jax.ShapeDtypeStruct(a.shape[1:], a.dtype) for a in pairs]
+    dma = pltpu.SemaphoreType.DMA
+    return pl.pallas_call(
+        functools.partial(gather_kernel, kinds, s, p),
+        out_shape=outs,
+        in_specs=[VMEM_SPEC] * (n + s + p),
+        out_specs=[ANY_SPEC] * (n + s + p),
+        scratch_shapes=[
+            dma((10, n, 4)),
+            dma((10, n, 4)),
+            dma((n,)),
+            dma((max(s, 1), 3, 2)),
+            dma((max(p, 1), 3)),
+        ],
+        compiler_params=pltpu.CompilerParams(collective_id=collective_id, has_side_effects=True),
+        name="gather",
+    )(*arrays, *swaps, *pairs)
+
+
+def scatter_kernel(kinds, swaps, *refs):
+    n = len(kinds)
+    srcs, refs = (refs[:n], refs[n:])
+    swap_in, refs = (refs[:swaps], refs[swaps:])
+    outs, refs = (refs[:n], refs[n:])
+    swap_out, refs = (refs[:swaps], refs[swaps:])
+    acc, refs = (refs[:n], refs[n:])
+    mate, refs = (refs[:n], refs[n:])
+    from_x, refs = (refs[:n], refs[n:])
+    from_y, refs = (refs[:n], refs[n:])
+    corner, refs = (refs[:n], refs[n:])
+    chain, refs = (refs[:n], refs[n:])
+    last, refs = (refs[:n], refs[n:])
+    send_sem, recv_sem, local_sem, swap_sem = refs
+    x, c, z, y = place()
+    nx, ny, partner = (device(1 - x, c, z, y), device(x, c, z, 1 - y), device(x, 1 - c, z, y))
+    up, down = (
+        device(x, c, jnp.minimum(z + 1, 3), y),
+        device(x, c, jnp.maximum(z - 1, 0), y),
+    )
+    peers = [(None, nx), (None, ny), (None, partner), (z > 0, down), (z < 3, up)]
+    if swaps:
+        peers += swap_peers()
+    greet(peers)
+    owners = ((x, y), (1 - x, y), (x, 1 - y), (1 - x, 1 - y))
+
+    def level(step):
+        side = z // 2
+        near = side * (3 - z) + (1 - side) * z
+        late = step // 2
+        base = (1 - late) * (3 - step) + late * ((1 - near) * (3 - step) + near * (step - 2))
+        return side * (3 - base) + (1 - side) * base
+
+    def shard(a, core, owner, k):
+        i = (owner[0] * 2 + core) * 8 + k * 2 + owner[1]
+        return srcs[a].at[:, i] if kinds[a] == "split" else srcs[a].at[i]
+
+    def half_of(ref, a, half):
+        if half and kinds[a] == "split":
+            return ref.at[0:2] if half == 1 else ref.at[2:4]
+        return ref
+
+    def load(a, k, q):
+        return pltpu.make_async_copy(shard(a, c, owners[q], k), acc[a].at[k, q], local_sem.at[a, k, q])
+
+    def over(a, k, q, core):
+        return remote(
+            shard(a, core, owners[q], k), mate[a].at[k, q], send_sem.at[q, a, k], recv_sem.at[q, a, k], partner
+        )
+
+    def hop(kind, a, k, q, half, target, to):
+        return remote(
+            half_of(acc[a].at[k, q], a, half),
+            half_of(target[a].at[k], a, half),
+            send_sem.at[kind, a, k],
+            recv_sem.at[kind, a, k],
+            to,
+        )
+
+    t_h1, t_h2, t_x, t_y, t_z, t_last = range(4, 10)
+
+    def begin(step, _):
+        k = level(step)
+        for q in (3, 1, 2, 0):
+            for a in range(n):
+                over(a, k, q, 1 - c).start()
+                load(a, k, q).start()
+        return 0
+
+    lax.fori_loop(0, 4, begin, 0)
+    moves = [
+        swap_copies(swap_in[i], swap_out[i], swap_sem.at[i, 0], swap_sem.at[i, 1], swap_sem.at[i, 2])
+        for i in range(swaps)
+    ]
+    for start, _ in moves:
+        start()
+
+    def wide(ref):
+        return ref[...].astype(jnp.float32)
+
+    def arrived(a, k, q):
+        load(a, k, q).wait()
+        over(a, k, q, c).wait_recv()
+
+    def first(step):
+        k = level(step)
+        for a in range(n):
+            arrived(a, k, 3)
+            here = acc[a].at[k, 3]
+            here[...] = (wide(here) + wide(mate[a].at[k, 3])).astype(jnp.bfloat16)
+            if a in half_members(kinds, 1):
+                hop(t_h1, a, k, 3, 1, corner, ny).start()
+            if a in half_members(kinds, 2):
+                hop(t_h2, a, k, 3, 2, corner, nx).start()
+
+    def second(step):
+        k = level(step)
+        for q, half, kind, target, to in (
+            (1, 1, t_h1, from_x, nx),
+            (2, 2, t_h2, from_y, ny),
+        ):
+            for a in range(n):
+                arrived(a, k, q)
+                here = acc[a].at[k, q]
+                here[...] = (wide(here) + wide(mate[a].at[k, q])).astype(jnp.bfloat16)
+                if a in half_members(kinds, half):
+                    hop(kind, a, k, 3, half, corner, to).wait_recv()
+                    part = half_of(here, a, half)
+                    part[...] = (wide(part) + wide(half_of(corner[a].at[k], a, half))).astype(
+                        jnp.bfloat16
+                    )
+                hop(t_x if q == 1 else t_y, a, k, q, 0, target, to).start()
+
+    def gathered(a, k):
+        arrived(a, k, 0)
+        hop(t_x, a, k, 1, 0, from_x, nx).wait_recv()
+        hop(t_y, a, k, 2, 0, from_y, ny).wait_recv()
+        return (
+            wide(acc[a].at[k, 0])
+            + wide(mate[a].at[k, 0])
+            + (wide(from_x[a].at[k]) + wide(from_y[a].at[k]))
+        )
+
+    def third(step):
+        k = level(step)
+        inner = jnp.logical_or(jnp.logical_and(k < z, z < 3), jnp.logical_and(k > z, z > 0))
+        for a in range(n):
+            here = acc[a].at[k, 0]
+            here[...] = gathered(a, k).astype(jnp.bfloat16)
+
+            @pl.when(inner)
+            def _(a=a, here=here):
+                hop(t_z, a, k, 0, 0, chain, up).wait_recv()
+                here[...] = (wide(here) + wide(chain[a].at[k])).astype(jnp.bfloat16)
+
+            def final_hop(to, kind, target, a=a):
+                return remote(
+                    acc[a].at[k, 0], target, send_sem.at[kind, a, k], recv_sem.at[kind, a, k], to
+                )
+
+            pl.when(k > z + 1)(final_hop(up, t_z, chain[a].at[k]).start)
+            pl.when(k < z - 1)(final_hop(down, t_z, chain[a].at[k]).start)
+            pl.when(k == z + 1)(final_hop(up, t_z, last[a].at[0]).start)
+            pl.when(k == z - 1)(final_hop(down, t_last, last[a].at[1]).start)
+
+    def body(step, _):
+        pl.when(step < 4)(lambda: first(step))
+        pl.when(jnp.logical_and(step >= 1, step < 5))(lambda: second(step - 1))
+        pl.when(step >= 2)(lambda: third(step - 2))
+        return 0
+
+    lax.fori_loop(0, 5, body, 0)
+    second_done = None
+    for a in range(n):
+        outs[a][...] = gathered(a, z)
+
+        @pl.when(z > 0)
+        def _(a=a):
+            remote(last[a].at[0], last[a].at[0], send_sem.at[t_z, a, z], recv_sem.at[t_z, a, z], up).wait_recv()
+            outs[a][...] += wide(last[a].at[0])
+
+        @pl.when(z < 3)
+        def _(a=a):
+            remote(
+                last[a].at[1], last[a].at[1], send_sem.at[t_last, a, z], recv_sem.at[t_last, a, z], up
+            ).wait_recv()
+            outs[a][...] += wide(last[a].at[1])
+
+    def finish(step, _):
+        k = level(step)
+        for a in range(n):
+            for q in range(4):
+                over(a, k, q, 1 - c).wait_send()
+            if a in half_members(kinds, 1):
+                hop(t_h1, a, k, 3, 1, corner, ny).wait_send()
+            if a in half_members(kinds, 2):
+                hop(t_h2, a, k, 3, 2, corner, nx).wait_send()
+            hop(t_x, a, k, 1, 0, from_x, nx).wait_send()
+            hop(t_y, a, k, 2, 0, from_y, ny).wait_send()
+
+            pl.when(jnp.logical_or(k > z, k < z - 1))(
+                hop(t_z, a, k, 0, 0, chain, up).wait_send
+            )
+            pl.when(k == z - 1)(
+                remote(
+                    acc[a].at[k, 0], last[a].at[1], send_sem.at[t_last, a, k], recv_sem.at[t_last, a, k], down
+                ).wait_send
+            )
+        return 0
+
+    lax.fori_loop(0, 4, finish, 0)
+    for _, wait in moves:
+        wait()
+
+
+def scatter(kinds, arrays, swaps, collective_id):
+    n, s = (len(arrays), len(swaps))
+    shards = []
+    for kind, array in zip(kinds, arrays):
+        shards.append(array.shape[:1] + array.shape[2:] if kind == "split" else array.shape[1:])
+    dma = pltpu.SemaphoreType.DMA
+    scratch = []
+    for lead in ((4, 4), (4, 4), (4,), (4,), (4,), (4,), (2,)):
+        scratch += [pltpu.VMEM(lead + shape, jnp.bfloat16) for shape in shards]
+    return pl.pallas_call(
+        functools.partial(scatter_kernel, kinds, s),
+        out_shape=[jax.ShapeDtypeStruct(shape, jnp.float32) for shape in shards]
+        + [jax.ShapeDtypeStruct(a.shape, a.dtype) for a in swaps],
+        in_specs=[ANY_SPEC] * (n + s),
+        out_specs=[VMEM_SPEC] * n + [ANY_SPEC] * s,
+        scratch_shapes=scratch
+        + [dma((10, n, 4)), dma((10, n, 4)), dma((n, 4, 4)), dma((max(s, 1), 3, 2))],
+        compiler_params=pltpu.CompilerParams(
+            collective_id=collective_id, has_side_effects=True, vmem_limit_bytes=60 * 1024 * 1024
+        ),
+        name="scatter",
+    )(*arrays, *swaps)
+
+
+def trade_kernel(to_heads, src, dst, send_sem, recv_sem, local_sem):
+    x, c, z, y = place()
+    others = ((y, 1 - c), (1 - y, c), (1 - y, 1 - c))
+    greet([(None, device(x, core, z, yy)) for yy, core in others])
+
+    def ends(yy, core, k, mine_y, mine_c):
+        if to_heads:
+            rows = (2 * mine_c + k) * 2 + mine_y
+            return (src.at[yy * 2 + core, k], dst.at[rows])
+        rows = (2 * core + k) * 2 + yy
+        return (src.at[rows], dst.at[mine_y * 2 + mine_c, k])
+
+    for k in range(2):
+        a, b = ends(y, c, k, y, c)
+        pltpu.make_async_copy(a, b, local_sem.at[k]).start()
+        for i, (yy, core) in reversed(list(enumerate(others))):
+            a, b = ends(yy, core, k, y, c)
+            remote(a, b, send_sem.at[i, k], recv_sem.at[i, k], device(x, core, z, yy)).start()
+    for k in range(2):
+        a, b = ends(y, c, k, y, c)
+        pltpu.make_async_copy(a, b, local_sem.at[k]).wait()
+        for i, (yy, core) in enumerate(others):
+            peer = device(x, core, z, yy)
+            a, b = ends(yy, core, k, y, c)
+            remote(a, b, send_sem.at[i, k], recv_sem.at[i, k], peer).wait_send()
+            a, b = ends(y, c, k, yy, core)
+            remote(b, b, send_sem.at[i, k], recv_sem.at[i, k], peer).wait_recv()
+
+
+def trade(array, to_heads, collective_id):
+    dma = pltpu.SemaphoreType.DMA
+    width = array.shape[-1]
+    shape = (8, 128, width) if to_heads else (4, 2, 128, width)
+    return pl.pallas_call(
+        functools.partial(trade_kernel, to_heads),
+        out_shape=jax.ShapeDtypeStruct(shape, array.dtype),
+        in_specs=[VMEM_SPEC],
+        out_specs=VMEM_SPEC,
+        scratch_shapes=[dma((3, 2)), dma((3, 2)), dma((2,))],
+        compiler_params=pltpu.CompilerParams(collective_id=collective_id, has_side_effects=True),
+        name="trade",
+    )(array)
+
+
+ROWS = 256
+MASKED = -1e30
+NT = (((1,), (1,)), ((), ()))
+TN = (((0,), (0,)), ((), ()))
+
+
+def mm(a, b, dims=(((1,), (0,)), ((), ()))):
+    return lax.dot_general(a, b, dims, preferred_element_type=jnp.float32)
+
+
+def angle_constants():
+    half = D // 2
+    inverse = 10000.0 ** (-np.arange(half, dtype=np.float64) / half)
+    inverse = inverse.astype(np.float32).astype(np.float64)
+    coarse = inverse[:, None] * (1023.0 - 128.0 * np.arange(16)[None, :])
+    fine = inverse[:, None] * np.arange(128.0)[None, :]
+    coarse_table = np.concatenate([np.sin(coarse), np.cos(coarse)], axis=0).astype(np.float32)
+    fine_table = np.concatenate([np.sin(fine), np.cos(fine)], axis=0).astype(np.float32)
+    return (coarse_table, fine_table)
+
+
+def position_kernel(coarse_ref, fine_ref, w_ref, table_ref, keys_ref):
+    half = D // 2
+    fine_sin = fine_ref[:half, :]
+    fine_cos = fine_ref[half:, :]
+    weight = w_ref[...]
+    for a in range(16):
+        big_sin = coarse_ref[:half, a : a + 1]
+        big_cos = coarse_ref[half:, a : a + 1]
+        sines = big_sin * fine_cos - big_cos * fine_sin
+        cosines = big_cos * fine_cos + big_sin * fine_sin
+        piece = jnp.concatenate([sines, cosines], axis=0).astype(jnp.bfloat16)
+        table_ref[:, a * 128 : (a + 1) * 128] = piece
+        keys_ref[:, a * 128 : (a + 1) * 128] = mm(weight, piece, TN).astype(jnp.bfloat16)
+
+
+def position_tables(w_pos):
+    coarse, fine = angle_constants()
+    return pl.pallas_call(
+        position_kernel,
+        out_shape=(
+            jax.ShapeDtypeStruct((D, 2048), jnp.bfloat16),
+            jax.ShapeDtypeStruct((192, 2048), jnp.bfloat16),
+        ),
+        name="positions",
+    )(jnp.asarray(coarse), jnp.asarray(fine), w_pos)
+
+
+def query_parts(q, vec, h, kind):
+    q = q.astype(jnp.float32)
+    lanes = slice(h * 64, h * 64 + 64)
+    content = (q + vec[0:1, lanes]).astype(jnp.bfloat16).astype(jnp.float32) * DH ** (-0.5)
+    position = (q + vec[1:2, lanes]).astype(jnp.bfloat16) * jnp.bfloat16(DH ** (-0.5))
+    typed = q + vec[2:3, lanes]
+    other = jnp.sum(typed * vec[3:4, lanes], axis=1, keepdims=True) * DH ** (-0.5)
+    same = jnp.sum(typed * vec[4:5, lanes], axis=1, keepdims=True) * DH ** (-0.5)
+    to_zero = jnp.where(kind > 0.5, other, same)
+    to_one = jnp.where(kind > 0.5, same, other)
+    return (content, position, typed, to_zero, to_one)
+
+
+def wide_query(content, to_zero, to_one, side):
+    rows = content.shape[0]
+    lane = lax.broadcasted_iota(jnp.int32, (rows, 64), 1)
+
+    def split(value):
+        high = value.astype(jnp.bfloat16).astype(jnp.float32)
+        return (high, value - high)
+
+    zero_high, zero_low = split(to_zero)
+    one_high, one_low = split(to_one)
+    extra = jnp.where(
+        lane == 0,
+        zero_high,
+        jnp.where(
+            lane == 1, one_high, jnp.where(lane == 2, zero_low, jnp.where(lane == 3, one_low, side))
+        ),
+    )
+    return jnp.concatenate([content, extra], axis=1).astype(jnp.bfloat16)
+
+
+def attend_kernel(qkv_ref, side_ref, key_side_ref, vec_ref, keys_ref, attn_ref, probs_ref, wide_key):
+    step = pl.program_id(0)
+    rows = ROWS
+    start = pl.multiple_of(step * rows, rows)
+    vec = vec_ref[...]
+
+    @pl.when(step == 0)
+    def _():
+        for h in range(3):
+            key = qkv_ref[:, 192 + h * 64 : 256 + h * 64]
+            wide_key[h] = jnp.concatenate([key, key_side_ref[...]], axis=1)
+
+    block = qkv_ref[pl.ds(start, rows), 0:192]
+    side = side_ref[pl.ds(start, rows), :].astype(jnp.float32)
+    kind = side[:, 0:1]
+    width = 1024 + rows
+    from_n = pl.multiple_of(1024 - rows - start, 128)
+    outs = []
+    for h in range(3):
+        content, position, _, to_zero, to_one = query_parts(
+            block[:, h * 64 : h * 64 + 64], vec, h, kind
+        )
+        query = wide_query(content, to_zero, to_one, side)
+        scores = mm(query, wide_key[h], NT)
+        slab = mm(position, keys_ref[h * 64 : h * 64 + 64, pl.ds(from_n, width)])
+        slab = pltpu.roll(slab, width - (rows - 1), 1, stride=1, stride_axis=0)
+        scores = scores + slab[:, :1024]
+        top = jnp.max(scores, axis=1, keepdims=True)
+        expo = jnp.exp(scores - top)
+        total = jnp.sum(expo, axis=1, keepdims=True)
+        probs = (expo * (1.0 / total)).astype(jnp.bfloat16)
+        probs_ref[h] = probs
+        outs.append(mm(probs, qkv_ref[:, 384 + h * 64 : 448 + h * 64]))
+    attn_ref[...] = jnp.concatenate(outs, axis=1).astype(jnp.bfloat16)
+
+
+def attend(qkv, side, key_side, vec, keys):
+    rows = ROWS
+    whole = lambda shape: pl.BlockSpec(shape, lambda i: (0,) * len(shape))
+    return pl.pallas_call(
+        attend_kernel,
+        grid=(1024 // rows,),
+        out_shape=(
+            jax.ShapeDtypeStruct((1024, 192), jnp.bfloat16),
+            jax.ShapeDtypeStruct((3, 1024, 1024), jnp.bfloat16),
+        ),
+        in_specs=[
+            whole((1024, 576)),
+            whole((1024, 64)),
+            whole((1024, 64)),
+            whole((8, 192)),
+            whole((192, 2048)),
+        ],
+        out_specs=(
+            pl.BlockSpec((rows, 192), lambda i: (i, 0)),
+            pl.BlockSpec((3, rows, 1024), lambda i: (0, i, 0)),
+        ),
+        scratch_shapes=[pltpu.VMEM((3, 1024, 128), jnp.bfloat16)],
+        compiler_params=pltpu.CompilerParams(vmem_limit_bytes=48 * 1024 * 1024),
+        name="attend",
+    )(qkv, side, key_side, vec, keys)
+
+
+def attend_back_kernel(
+    qkv_ref,
+    side_ref,
+    key_side_ref,
+    vec_ref,
+    keys_ref,
+    probs_ref,
+    attn_ref,
+    grad_ref,
+    out_ref,
+    grad_keys_ref,
+    grad_vec_ref,
+    wide_key,
+    grad_key,
+    grad_value,
+    grad_table,
+):
+    step = pl.program_id(0)
+    rows = ROWS
+    start = pl.multiple_of(step * rows, rows)
+    vec = vec_ref[...]
+
+    @pl.when(step == 0)
+    def _():
+        for h in range(3):
+            key = qkv_ref[:, 192 + h * 64 : 256 + h * 64]
+            wide_key[h] = jnp.concatenate([key, key_side_ref[...]], axis=1)
+        grad_key[...] = jnp.zeros_like(grad_key)
+        grad_value[...] = jnp.zeros_like(grad_value)
+        grad_table[...] = jnp.zeros_like(grad_table)
+        grad_vec_ref[...] = jnp.zeros_like(grad_vec_ref)
+
+    block = qkv_ref[pl.ds(start, rows), 0:192]
+    side = side_ref[pl.ds(start, rows), :].astype(jnp.float32)
+    kind = side[:, 0:1]
+    width = 1024 + rows
+    from_n = pl.multiple_of(1024 - rows - start, 128)
+    scale = DH ** (-0.5)
+    grads = grad_ref[...]
+    outs = attn_ref[...].astype(jnp.float32)
+    grad_queries = []
+    row = lax.broadcasted_iota(jnp.int32, (rows, rows), 0)
+    column = lax.broadcasted_iota(jnp.int32, (rows, rows), 1)
+    reverse = jnp.where(row + column == rows - 1, 1.0, 0.0).astype(jnp.bfloat16)
+    for h in range(3):
+        lanes = slice(h * 64, h * 64 + 64)
+        content, position, typed, _, _ = query_parts(block[:, lanes], vec, h, kind)
+        probs = probs_ref[h]
+        grad = grads[:, lanes]
+        delta = jnp.sum(outs[:, lanes] * grad.astype(jnp.float32), axis=1, keepdims=True)
+        grad_probs = mm(grad, qkv_ref[:, 384 + h * 64 : 448 + h * 64], NT)
+        grad_value[h] += mm(probs, grad, TN)
+        grad_scores = probs.astype(jnp.float32) * (grad_probs - delta)
+        low = grad_scores.astype(jnp.bfloat16)
+        grad_key[h] += mm(low, content.astype(jnp.bfloat16), TN)
+        grad_wide = mm(low, wide_key[h])
+        turned = mm(reverse, low)
+        padded = jnp.concatenate([turned, jnp.zeros((rows, rows), jnp.float32)], axis=1)
+        skew = pltpu.roll(padded, 0, 1, stride=1, stride_axis=0).astype(jnp.bfloat16)
+        slab = keys_ref[lanes, pl.ds(from_n, width)]
+        turned = mm(skew, slab, NT) * scale
+        high = turned.astype(jnp.bfloat16)
+        rest = (turned - high.astype(jnp.float32)).astype(jnp.bfloat16)
+        grad_position = mm(reverse, high) + mm(reverse, rest)
+        position = mm(reverse, position).astype(jnp.bfloat16)
+        grad_table[lanes, pl.ds(from_n, width)] += mm(position, skew, TN)
+        grad_content = grad_wide[:, :64] * scale
+        to_zero = grad_wide[:, 64:65] * scale
+        to_one = grad_wide[:, 65:66] * scale
+        same = jnp.where(kind > 0.5, to_one, to_zero)
+        other = jnp.where(kind > 0.5, to_zero, to_one)
+        grad_typed = other * vec[3:4, lanes] + same * vec[4:5, lanes]
+        total = lambda value: jnp.sum(value, axis=0, keepdims=True)
+        grad_vec_ref[:, lanes] += jnp.concatenate(
+            [
+                total(grad_content),
+                total(grad_position),
+                total(grad_typed),
+                total(other * typed),
+                total(same * typed),
+                jnp.zeros((3, 64), jnp.float32),
+            ],
+            axis=0,
+        )
+        grad_queries.append(grad_content + grad_position + grad_typed)
+    out_ref[pl.ds(start, rows), 0:192] = jnp.concatenate(grad_queries, axis=1).astype(jnp.bfloat16)
+
+    @pl.when(step == 1024 // rows - 1)
+    def _():
+        out_ref[:, 192:384] = jnp.concatenate([grad_key[h] for h in range(3)], axis=1).astype(
+            jnp.bfloat16
+        )
+        out_ref[:, 384:576] = jnp.concatenate([grad_value[h] for h in range(3)], axis=1).astype(
+            jnp.bfloat16
+        )
+        grad_keys_ref[...] = grad_table[...].astype(jnp.bfloat16)
+
+
+def attend_back(qkv, side, key_side, vec, keys, probs, attn, grad):
+    rows = ROWS
+    whole = lambda shape: pl.BlockSpec(shape, lambda i: (0,) * len(shape))
+    return pl.pallas_call(
+        attend_back_kernel,
+        grid=(1024 // rows,),
+        out_shape=(
+            jax.ShapeDtypeStruct((1024, 576), jnp.bfloat16),
+            jax.ShapeDtypeStruct((192, 2048), jnp.bfloat16),
+            jax.ShapeDtypeStruct((8, 192), jnp.float32),
+        ),
+        in_specs=[
+            whole((1024, 576)),
+            whole((1024, 64)),
+            whole((1024, 64)),
+            whole((8, 192)),
+            whole((192, 2048)),
+            pl.BlockSpec((3, rows, 1024), lambda i: (0, i, 0)),
+            pl.BlockSpec((rows, 192), lambda i: (i, 0)),
+            pl.BlockSpec((rows, 192), lambda i: (i, 0)),
+        ],
+        out_specs=(whole((1024, 576)), whole((192, 2048)), whole((8, 192))),
+        scratch_shapes=[
+            pltpu.VMEM((3, 1024, 128), jnp.bfloat16),
+            pltpu.VMEM((3, 1024, 64), jnp.float32),
+            pltpu.VMEM((3, 1024, 64), jnp.float32),
+            pltpu.VMEM((192, 2048), jnp.float32),
+        ],
+        compiler_params=pltpu.CompilerParams(vmem_limit_bytes=56 * 1024 * 1024),
+        name="attend_back",
+    )(qkv, side, key_side, vec, keys, probs, attn, grad)
+
+
+def document_sides(seg_row, type_row):
+    length = seg_row.shape[0]
+    own = (seg_row[:, None] == jnp.arange(8, dtype=jnp.int32)[None, :]).astype(jnp.float32)
+    kind = type_row.astype(jnp.float32)[:, None]
+    pad = jnp.zeros((length, 52), jnp.float32)
+    side = jnp.concatenate([kind, kind, kind, kind, own, pad], axis=1).astype(jnp.bfloat16)
+    key_side = jnp.concatenate(
+        [1.0 - kind, kind, 1.0 - kind, kind, (1.0 - own) * MASKED, pad], axis=1
+    ).astype(jnp.bfloat16)
+    return (side, key_side)
+
+
+KINDS = ("split", 1, 1, 2, 1, 2)
+
+
+def sequence_device(
+    tokens,
+    seg_ids,
+    token_types,
+    attn_in,
+    attn_out,
+    pos_kernel,
+    ffn_in,
+    ffn_out,
+    head_vectors,
+    norm_gains,
+    norm_shifts,
+    out_bias,
+    ffn_bias,
+    cotangent,
+):
+    x, c, z, y = place()
+    group = y * 2 + c
+    low = jnp.bfloat16
+    w_in_shard = attn_in.reshape(24, 3, 4, 192).transpose(2, 0, 1, 3).reshape(4, 24, 576)
+    small = jnp.concatenate(
+        [
+            head_vectors,
+            norm_gains,
+            norm_shifts,
+            out_bias,
+            ffn_bias.reshape(4, 24),
+            jnp.zeros((1, 24), low),
+        ],
+        axis=0,
+    )
+    small = jnp.pad(small, ((0, 0), (0, 104)))
+    labels = jnp.stack([seg_ids, token_types], axis=1)
+    w_in, w_pos, vectors, w_out, w_up, w_down, rows, cot, label = gather(
+        KINDS,
+        [w_in_shard, pos_kernel, small, attn_out, ffn_in, ffn_out],
+        [tokens, cotangent],
+        [labels],
+        0,
+    )
+    w_in = w_in.reshape(4, D, 576)
+    w_pos = w_pos.reshape(D, HD)
+    w_out = w_out.reshape(HD, D)
+    w_up = w_up.reshape(D, FF)
+    w_down = w_down.reshape(FF, D)
+    rows = rows.reshape(256, D)
+    cot = cot.reshape(256, D)
+    vectors_f = vectors[:, :, :24].astype(jnp.float32)
+    up_bias = vectors_f[:, 11:15, :].reshape(FF)
+    vectors_f = vectors_f.transpose(1, 0, 2).reshape(16, D)
+    gains_f, shifts_f, biases_f = (vectors_f[5:7], vectors_f[7:9], vectors_f[9:11])
+    w_pos_own = lax.dynamic_slice_in_dim(w_pos, group * 192, 192, axis=1)
+    vec = jnp.pad(
+        lax.dynamic_slice_in_dim(vectors_f[:5], group * 192, 192, axis=1), ((0, 3), (0, 0))
+    )
+    side, key_side = document_sides(label[0], label[1])
+
+    proj = jnp.einsum("id,tdk->tik", rows, w_in, preferred_element_type=jnp.float32).astype(low)
+    qkv = trade(proj.reshape(4, 2, 128, 576), True, 1).reshape(1024, 576)
+    table, keys = position_tables(w_pos_own)
+    attn_heads, probs = attend(qkv, side, key_side, vec, keys)
+    attn = trade(attn_heads.reshape(8, 128, 192), False, 2)
+    attn = attn.reshape(4, 256, 192).transpose(1, 0, 2).reshape(256, HD)
+    rows_f = rows.astype(jnp.float32)
+    branch = jnp.dot(attn, w_out, preferred_element_type=jnp.float32) + biases_f[0]
+    first, normed_one, inv_one = layer_norm(rows_f + branch, gains_f[0], shifts_f[0])
+    first_b = first.astype(low)
+    pre_act = jnp.dot(first_b, w_up, preferred_element_type=jnp.float32) + up_bias
+    hidden = gelu_tanh(pre_act).astype(low)
+    second = jnp.dot(hidden, w_down, preferred_element_type=jnp.float32) + biases_f[1]
+    result, normed_two, inv_two = layer_norm(first + second, gains_f[1], shifts_f[1])
+    result = result.astype(low)
+
+    grad_two = cot.astype(jnp.float32)
+    gain_two = jnp.sum(grad_two * normed_two, axis=0)
+    shift_two = jnp.sum(grad_two, axis=0)
+    grad_h2 = norm_back(grad_two, normed_two, inv_two, gains_f[1])
+    grad_second = grad_h2.astype(low)
+    bias_two = jnp.sum(grad_second.astype(jnp.float32), axis=0)
+    g_down = jnp.einsum("rf,rd->fd", hidden, grad_second, preferred_element_type=jnp.float32)
+    grad_hidden = jnp.einsum("rd,fd->rf", grad_second, w_down, preferred_element_type=jnp.float32)
+    grad_pre = jax.vjp(gelu_tanh, pre_act)[1](grad_hidden)[0].astype(low)
+    g_upbias = jnp.sum(grad_pre.astype(jnp.float32), axis=0)
+    g_up = jnp.einsum("rd,rf->df", first_b, grad_pre, preferred_element_type=jnp.float32)
+    grad_first = grad_h2 + jnp.einsum(
+        "rf,df->rd", grad_pre, w_up, preferred_element_type=jnp.float32
+    )
+    gain_one = jnp.sum(grad_first * normed_one, axis=0)
+    shift_one = jnp.sum(grad_first, axis=0)
+    grad_h1 = norm_back(grad_first, normed_one, inv_one, gains_f[0])
+    grad_branch = grad_h1.astype(low)
+    bias_one = jnp.sum(grad_branch.astype(jnp.float32), axis=0)
+    g_out = jnp.einsum("rk,rd->kd", attn, grad_branch, preferred_element_type=jnp.float32)
+    grad_attn = jnp.einsum(
+        "rd,tkd->trk", grad_branch, w_out.reshape(4, 192, D), preferred_element_type=jnp.float32
+    ).astype(low)
+
+    grad_heads = trade(grad_attn.reshape(4, 2, 128, 192), True, 3).reshape(1024, 192)
+    grad_qkv, grad_keys, grad_vec = attend_back(
+        qkv, side, key_side, vec, keys, probs, attn_heads, grad_heads
+    )
+    grad_proj = trade(grad_qkv.reshape(8, 128, 576), False, 4).reshape(4, 256, 576)
+    g_in = jnp.einsum("id,tik->tdk", rows, grad_proj, preferred_element_type=jnp.float32)
+    grad_x = grad_h1 + jnp.einsum(
+        "tik,tdk->id", grad_proj, w_in, preferred_element_type=jnp.float32
+    )
+    g_pos = jnp.einsum("cn,kn->ck", table, grad_keys, preferred_element_type=jnp.float32)
+    own = (jnp.arange(4) == group).astype(jnp.float32)[None, :, None]
+    g_pos = (g_pos[:, None, :] * own).reshape(D, HD).astype(low)
+    g_head = (grad_vec[:5, None, :] * own).reshape(5, HD)
+    g_small = jnp.concatenate(
+        [
+            g_head,
+            jnp.stack([gain_one, gain_two, shift_one, shift_two, bias_one, bias_two]),
+        ],
+        axis=0,
+    )
+    g_small = jnp.concatenate(
+        [
+            g_small.reshape(11, 32, 24).transpose(1, 0, 2),
+            g_upbias.reshape(32, 4, 24),
+            jnp.zeros((32, 1, 24), jnp.float32),
+        ],
+        axis=1,
+    )
+    g_small = jnp.pad(g_small, ((0, 0), (0, 0), (0, 104))).astype(low)
+    f_in, f_pos, f_small, f_out, f_up, f_down, out_rows, grad_rows = scatter(
+        KINDS,
+        [
+            g_in.astype(low).reshape(4, 32, 24, 576),
+            g_pos.reshape(32, 24, HD),
+            g_small,
+            g_out.astype(low).reshape(32, 24, D),
+            g_up.astype(low).reshape(32, 24, FF),
+            g_down.astype(low).reshape(32, 96, D),
+        ],
+        [result.reshape(2, 128, D), grad_x.astype(low).reshape(2, 128, D)],
+        5,
+    )
+    f_in = f_in.reshape(4, 24, 3, 192).transpose(1, 2, 0, 3).reshape(24, 3 * HD)
+    f_small = f_small[:, :24]
+    return (
+        out_rows,
+        grad_rows.astype(jnp.float32),
+        f_in,
+        f_out,
+        f_pos,
+        f_up,
+        f_down,
+        f_small[0:5],
+        f_small[5:7],
+        f_small[7:9],
+        f_small[9:11],
+        f_small[11:15].reshape(96),
+    )
+
+
 def solution(mesh):
     placed = (
         P("dp", "fsdp", None),
@@ -414,8 +1419,9 @@
         P(("dp", "fsdp")),
         P("dp", "fsdp", None),
     )
+    two_by_four = tuple(mesh.shape[name] for name in ("dp", "fsdp")) == (4, 8)
     return jax.shard_map(
-        per_device,
+        sequence_device if two_by_four else per_device,
         mesh=mesh,
         in_specs=placed,
         out_specs=(

time: 1430 us -> 373 us (0.26)
  waiting for transfers between devices: 755 us -> 0 us
  blocking collectives: 342 us -> 0 us
  Pallas kernels: 0 us -> 268 us
  matrix products: 165 us -> 37.5 us
  local copies, waits for them, and re-layouts: 101 us -> 45.9 us
  other arithmetic: 42.4 us -> 13.5 us
  between operations: 16.4 us -> 1.51 us
    reduce_scatter x4 -> x0, waiting for transfers between devices: 366 us -> none  [the longest x1 142 us: per_device(): lax.psum_scatter(totals[4], ('dp', 'fsdp'), scatter_dimension=0, tiled=True)]
    unnamed x23 -> x0, waiting for transfers between devices: 306 us -> none
    pallas_call x0 -> x9, Pallas kernels: none -> 268 us  [the longest x1 80.5 us: gather(): pl.pallas_call(functools.partial(gather_kernel, kinds, s, p), out_shape=o...]
    all_gather x4 -> x0, blocking collectives: 262 us -> none  [the longest x1 66.3 us: fetch_forward(): lax.all_gather(shards[5], ('dp', 'fsdp'), axis=1, tiled=True)]
    dot_general x50 -> x13, matrix products: 140 us -> 37.5 us  [the longest x1 6.39 us: sequence_device(): jnp.einsum('rf,rd->fd', hidden, grad_second, preferred_element_type=jnp.f...]
    all_gather x9 -> x0, waiting for transfers between devices: 83.5 us -> none  [the longest x1 65 us: fetch_forward(): lax.all_gather(shards[0], ('dp', 'fsdp'), axis=0, tiled=True)]
    unnamed x2 -> x0, blocking collectives: 79.6 us -> none
    unnamed x267 -> x85, local copies, waits for them, and re-layouts: 40.4 us -> 6.88 us
  transfers between devices with their start and end apart: 18 -> 0, of which waited for: 9 -> 0; matrix products, arithmetic and copies ran while one was open for 18% -> 0% of each run, Pallas kernels for 0% -> 0%
where the time goes in v1:
time: 373 us; the launch traced here: 367 us
  Pallas kernels  268 us (72%)
  local copies, waits for them, and re-layouts  45.9 us (12%)
  matrix products  37.5 us (10%)
  other arithmetic  13.5 us (4%)
    pallas_call x1, Pallas kernels, gather(): pl.pallas_call(functools.partial(gather_kernel, kinds, s, p), out_shape=o...  80.5 us
    pallas_call x1, Pallas kernels, scatter(): pl.pallas_call(functools.partial(scatter_kernel, kinds, s), out_shape=[ja...  75.2 us
    pallas_call x4, Pallas kernels, trade(): pl.pallas_call(functools.partial(trade_kernel, to_heads), out_shape=jax.S...  61.2 us
    pallas_call x1, Pallas kernels, attend_back(): pl.pallas_call(attend_back_kernel, grid=(1024 // rows,), out_shape=(jax.S...  28.8 us
    pallas_call x1, Pallas kernels, attend(): pl.pallas_call(attend_kernel, grid=(1024 // rows,), out_shape=(jax.ShapeD...  16.7 us

profile of v1, /device:TPU:0, one launch (start us, length us, event | category | flops | bytes accessed | tf_op | source)
XLA Modules:
  0.0 366.6 jit_solution(8301919975683415626)
XLA Ops:
  2.7 2.1 concatenate.32
  8.2 1.1 reshape.248
  9.3 0.8 reshape.249.refs_0_
  10.2 80.5 %gather.1 = (bf16[4,32,24,576]{3,2,1,0:T(8,128)(2,1)}, bf16[32,24,768]{2,1,0:T(8,128)(2,1)}, bf16[32,16,128]{2,1,0:T(8,128)(2,1)}, bf16[32,24,768]{2,1,0:T(8,128...) custom-call(bf16[4,24,576]{2,1,0:T(8,128)(2,1)} %reshape.249.refs_0_, ...), custom_call_target="tpu_custom_call" | custom-call | tf_op jit(solution)/shard_map/gather/pallas_call | solution.py:678
  90.7 1.1 reduce.2
  92.5 0.8 fusion.38
  94.7 0.9 concatenate.34.key_side_ref
  96.6 2.1 constant_dynamic-slice_fusion.w_ref
  102.4 3.5 fusion.7
  105.9 1.5 copy.94
  107.3 20.2 %trade.4 = bf16[8,128,576]{2,1,0:T(8,128)(2,1)} custom-call(bf16[4,2,128,576]{3,2,1,0:T(8,128)(2,1)} %bitcast.104), custom_call_target="tpu_custom_call" | custom-call | tf_op jit(solution)/shard_map/trade/pallas_call | solution.py:947
  127.6 5.7 %positions.1 = (bf16[768,2048]{1,0:T(8,128)(2,1)}, bf16[192,2048]{1,0:T(8,128)(2,1)}) custom-call(f32[768,16]{1,0:T(8,128)} %constant.67.clone.coarse_ref, f32[768,128]{1,0:T(8,128)} %constant.68.clone.fine_ref, bf16[768,192]{1,0:T(8,128)(2,1)} %constant_dynamic-slice_fusion.w_ref), custom_call_target="tpu_custom_call" | custom-call | tf_op jit(solution)/shard_map/positions/pallas_call | solution.py:996
  133.3 1.3 copy-done
  134.6 1.1 copy-done.1
  135.8 16.7 %attend.1 = (bf16[1024,192]{1,0:T(8,128)(2,1)S(1)}, bf16[3,1024,1024]{2,1,0:T(8,128)(2,1)}) custom-call(bf16[1024,576]{1,0:T(8,128)(2,1)S(1)} %bitcast.99, bf16[1024,64]{1,0:T(8,128)(2,1)S(1)} %concatenate.33.side_ref, bf16[1024,64]{1,0:T(8,128)(2,1)S(1)} %concatenate.34.key_side_ref, f32[8,192]{1,0:T(8,128)S(1)} %pad.14.vec_ref, bf16[192,2048]{1,0:T(8,128)(2,1)S(1)} %copy-done.1), custom_call_target="tpu_custom_call" | custom-call | tf_op jit(solution)/shard_map/attend/pallas_call | solution.py:1078
  152.5 0.8 copy-done.4
  153.3 10.7 %trade.5 = bf16[4,2,128,192]{3,2,1,0:T(8,128)(2,1)} custom-call(bf16[8,128,192]{2,1,0:T(8,128)(2,1)} %bitcast.100), custom_call_target="tpu_custom_call" | custom-call | tf_op jit(solution)/shard_map/trade/pallas_call | solution.py:947
  164.0 1.2 copy.105
  166.1 4.0 %convolution_add_fusion = f32[256,3072]{1,0:T(8,128)S(1)} fusion(bf16[768,3072]{1,0:T(8,128)(2,1)} %bitcast.126, f32[3072]{0:T(1024)S(1)} %copy-done.27, f32[256,768]{1,0:T(8,128)S(1)} %get-tuple-element.85, f32[768]{0:T(1024)S(1)} %add.116, f32[768]{0:T(1024)S(1)} %mul.217, f32[256]{0:T(256)S(1)} %add_rsqrt_fusion.1, f32[256]{0:T(256)S(1)} %broadcast_multiply_fusion.4), kind=kOutput, calls=%fused_computation.7 | convolution fusion | flops 1209729024 | bytes 8671232 | tf_op jit(solution)/shard_map/dot_general | solution.py:1315
  170.2 2.1 fusion.40
  172.5 1.7 fusion.19
  174.3 0.9 convert_reduce_fusion.1
  175.2 4.3 %fusion.41 = (bf16[3072]{0:T(1024)(128)(2,1)}, bf16[256,3072]{1,0:T(8,128)(2,1)S(1)}) fusion(f32[256,3072]{1,0:T(8,128)S(1)} %convolution_add_fusion, bf16[3072,768]{1,0:T(8,128)(2,1)S(1)} %bitcast.133, f32[256,768]{1,0:T(8,128)S(1)} %get-tuple-element.73), kind=kOutput, calls=%fused_computation.95 | convolution fusion | flops 1227813888 | bytes 10229760 | tf_op jit(solution)/shard_map/rd,fd->rf/dot_general | solution.py:1328
  179.5 2.2 multiply_reduce_fusion
  181.7 0.9 convert_reduce_fusion
  183.9 0.8 concatenate.43
  184.7 0.8 concatenate.48
  186.3 0.8 reshape.266
  187.1 1.0 copy.106
  188.1 10.7 %trade.6 = bf16[8,128,192]{2,1,0:T(8,128)(2,1)} custom-call(bf16[4,2,128,192]{3,2,1,0:T(8,128)(2,1)} %bitcast.112), custom_call_target="tpu_custom_call" | custom-call | tf_op jit(solution)/shard_map/trade/pallas_call | solution.py:947
  198.8 28.8 %attend_back.1 = (bf16[1024,576]{1,0:T(8,128)(2,1)}, bf16[192,2048]{1,0:T(8,128)(2,1)}, f32[8,192]{1,0:T(8,128)}) custom-call(bf16[1024,576]{1,0:T(8,128)(2,1)} %bitcast.98, bf16[1024,64]{1,0:T(8,128)(2,1)} %copy-done.3, bf16[1024,64]{1,0:T(8,128)(2,1)} %copy-done.2, f32[8,192]{1,0:T(8,128)} %copy-done.5, bf16[192,2048]{1,0:T(8,128)(2,1)} %get-tuple-element.41.keys_ref, ...), custom_call_target="tpu_custom_call" | custom-call | tf_op jit(solution)/shard_map/attend_back/pallas_call | solution.py:1203
  227.6 3.0 fusion.42
  230.7 19.7 %trade.7 = bf16[4,2,128,576]{3,2,1,0:T(8,128)(2,1)} custom-call(bf16[8,128,576]{2,1,0:T(8,128)(2,1)} %bitcast.118), custom_call_target="tpu_custom_call" | custom-call | tf_op jit(solution)/shard_map/trade/pallas_call | solution.py:947
  250.4 4.5 %fusion.11 = bf16[256,768]{1,0:T(8,128)(2,1)} fusion(f32[256,768]{1,0:T(8,128)S(1)} %get-tuple-element.75, bf16[4,256,576]{2,1,0:T(8,128)(2,1)} %bitcast.103, bf16[4,768,576]{2,1,0:T(8,128)(2,1)} %bitcast.135), kind=kOutput, calls=%fused_computation.27 | convolution fusion | flops 906362880 | bytes 5898240 | tf_op jit(solution)/shard_map/tik,tdk->id/dot_general | solution.py:1351
  255.0 1.5 convolution_convert_fusion.2
  257.7 6.4 %convolution_convert_fusion = bf16[3072,768]{1,0:T(8,128)(2,1)} fusion(f32[256,768]{1,0:T(8,128)S(1)} %copy-done.14, f32[256,3072]{1,0:T(8,128)} %copy-done.35), kind=kOutput, calls=%fused_computation.1 | convolution fusion | flops 1217593344 | bytes 8650752 | tf_op jit(solution)/shard_map/rf,rd->fd/dot_general | solution.py:1327
  264.1 3.8 %convolution_convert_fusion.1 = bf16[768,3072]{1,0:T(8,128)(2,1)} fusion(bf16[256,3072]{1,0:T(8,128)(2,1)S(1)} %copy-done.12, f32[256,768]{1,0:T(8,128)S(1)} %get-tuple-element.85, f32[768]{0:T(1024)S(1)} %add.116, f32[768]{0:T(1024)S(1)} %mul.217, f32[256]{0:T(256)S(1)} %copy-done.26, f32[256]{0:T(256)S(1)} %broadcast_multiply_fusion.4), kind=kOutput, calls=%fused_computation.2 | convolution fusion | flops 1211301888 | bytes 7086080 | tf_op jit(solution)/shard_map/rd,rf->df/dot_general | solution.py:1331
  268.4 3.1 mul.255
  271.5 3.0 multiply_convert_fusion.1.refs_1_
  274.5 1.2 fusion
  275.7 3.9 %copy.108 = bf16[4,768,576]{2,1,0:T(8,128)(2,1)} copy(bf16[4,768,576]{1,2,0:T(8,128)(2,1)S(1)} %fusion) | data formatting | bytes 7077888 | tf_op jit(solution)/shard_map/convert_element_type | solution.py:1377
  279.6 75.2 %scatter.1 = (f32[4,24,576]{2,1,0:T(8,128)}, f32[24,768]{1,0:T(8,128)}, f32[16,128]{1,0:T(8,128)}, f32[24,768]{1,0:T(8,128)}, f32[24,3072]{1,0:T(8,128)}, /*inde...) custom-call(bf16[4,32,24,576]{3,2,1,0:T(8,128)(2,1)} %bitcast.102, ...), custom_call_target="tpu_custom_call" | custom-call | tf_op jit(solution)/shard_map/scatter/pallas_call | solution.py:899
  354.9 0.8 slice.97
  356.2 1.3 fusion.37
  357.6 1.3 slice.93
  358.8 1.1 reshape.273
  360.1 0.9 reshape.274
  361.0 1.9 convert_element_type.145
  (144 shorter events, 21.4 us)
Async XLA Ops:
  90.7 8.0 %copy-start.19 = (bf16[32,16,128]{2,1,0:T(8,128)(2,1)S(1)}, bf16[32,16,128]{2,1,0:T(8,128)(2,1)}, u32[]{:S(2)}) copy-start(bf16[32,16,128]{2,1,0:T(8,128)(2,1)} %get-tuple-element.39) | copy-start | bytes 393220
  94.7 6.2 %copy-start.6 = (bf16[2,128,768]{2,1,0:T(8,128)(2,1)S(1)}, bf16[2,128,768]{2,1,0:T(8,128)(2,1)}, u32[]{:S(2)}) copy-start(bf16[2,128,768]{2,1,0:T(8,128)(2,1)} %get-tuple-element.47) | copy-start | bytes 1179652
  94.7 7.8 %copy-start.9 = (bf16[2,128,768]{2,1,0:T(8,128)(2,1)S(1)}, bf16[2,128,768]{2,1,0:T(8,128)(2,1)}, u32[]{:S(2)}) copy-start(bf16[2,128,768]{2,1,0:T(8,128)(2,1)} %get-tuple-element.37) | copy-start | bytes 1179652
  95.6 37.7 %copy-start.2 = (bf16[1024,64]{1,0:T(8,128)(2,1)}, bf16[1024,64]{1,0:T(8,128)(2,1)S(1)}, u32[]{:S(2)}) copy-start(bf16[1024,64]{1,0:T(8,128)(2,1)S(1)} %concatenate.34.key_side_ref) | copy-start | bytes 393220
  96.6 36.7 %copy-start.3 = (bf16[1024,64]{1,0:T(8,128)(2,1)}, bf16[1024,64]{1,0:T(8,128)(2,1)S(1)}, u32[]{:S(2)}) copy-start(bf16[1024,64]{1,0:T(8,128)(2,1)S(1)} %concatenate.33.side_ref) | copy-start | bytes 393220
  100.0 33.3 %copy-start.5 = (f32[8,192]{1,0:T(8,128)}, f32[8,192]{1,0:T(8,128)S(1)}, u32[]{:S(2)}) copy-start(f32[8,192]{1,0:T(8,128)S(1)} %pad.14.vec_ref) | copy-start | bytes 18436
  127.5 37.7 %copy-start.8 = (bf16[32,24,768]{2,1,0:T(8,128)(2,1)S(1)}, bf16[32,24,768]{2,1,0:T(8,128)(2,1)}, u32[]{:S(2)}) copy-start(bf16[32,24,768]{2,1,0:T(8,128)(2,1)} %get-tuple-element.44) | copy-start | bytes 3538948
  133.3 1.3 copy-start
  134.6 1.1 copy-start.1
  152.5 0.8 copy-start.4
  153.3 12.8 %copy-start.27 = (f32[3072]{0:T(1024)S(1)}, f32[3072]{0:T(1024)}, u32[]{:S(2)}) copy-start(f32[3072]{0:T(1024)} %add.119) | copy-start | bytes 36868
  165.9 4.3 %slice-start.2 = ((s8[4718592]{0:T(1024)(128)(4,1)}), s8[4194304]{0:T(1024)(128)(4,1)S(1)}, s32[]{:S(2)}) async-start(s8[4718592]{0:T(1024)(128)(4,1)} %bitcast.130), calls=%async_computation.2 | async-start | bytes 8388608
  166.1 15.6 %copy-start.25 = (f32[256]{0:T(256)}, f32[256]{0:T(256)S(1)}, u32[]{:S(2)}) copy-start(f32[256]{0:T(256)S(1)} %add_rsqrt_fusion.1) | copy-start | bytes 3076
  166.1 4.0 %copy-start.31 = (f32[768]{0:T(1024)S(1)}, f32[768]{0:T(1024)}, u32[]{:S(2)}) copy-start(f32[768]{0:T(1024)} %add.124) | copy-start | bytes 9220
  166.1 4.0 %slice-start.3 = ((s8[4718592]{0:T(1024)(128)(4,1)}), s8[524288]{0:T(1024)(128)(4,1)S(1)}, s32[]{:S(2)}) async-start(s8[4718592]{0:T(1024)(128)(4,1)} %bitcast.130), calls=%async_computation.3 | async-start | bytes 1048576
  170.1 5.0 %copy-start.35 = (f32[256,3072]{1,0:T(8,128)}, f32[256,3072]{1,0:T(8,128)S(1)}, u32[]{:S(2)}) copy-start(f32[256,3072]{1,0:T(8,128)S(1)} %convolution_add_fusion) | copy-start | bytes 9437188
  170.2 2.3 copy-start.23
  170.2 4.1 %copy-start.30 = (f32[256]{0:T(256)S(1)}, f32[256]{0:T(256)}, u32[]{:S(2)}) copy-start(f32[256]{0:T(256)} %multiply_bitcast_fusion) | copy-start | bytes 3076
  174.3 5.2 %slice-start = ((s8[4718592]{0:T(1024)(128)(4,1)}), s8[4194304]{0:T(1024)(128)(4,1)S(1)}, s32[]{:S(2)}) async-start(s8[4718592]{0:T(1024)(128)(4,1)} %bitcast.127), calls=%async_computation | async-start | bytes 8388608
  175.2 4.3 %copy-start.13 = (f32[256,768]{1,0:T(8,128)}, f32[256,768]{1,0:T(8,128)S(1)}, u32[]{:S(2)}) copy-start(f32[256,768]{1,0:T(8,128)S(1)} %get-tuple-element.73) | copy-start | bytes 2359300
  175.2 4.3 %slice-start.1 = ((s8[4718592]{0:T(1024)(128)(4,1)}), s8[524288]{0:T(1024)(128)(4,1)S(1)}, s32[]{:S(2)}) async-start(s8[4718592]{0:T(1024)(128)(4,1)} %bitcast.127), calls=%async_computation.1 | async-start | bytes 1048576
  179.5 2.3 copy-start.11
  181.7 3.7 %copy-start.28 = (bf16[768]{0:T(1024)(128)(2,1)S(1)}, bf16[768]{0:T(1024)(128)(2,1)}, u32[]{:S(2)}) copy-start(bf16[768]{0:T(1024)(128)(2,1)} %get-tuple-element.62) | copy-start | bytes 4612
  198.8 28.8 %copy-start.34 = (bf16[768,2048]{1,0:T(8,128)(2,1)S(1)}, bf16[768,2048]{1,0:T(8,128)(2,1)}, u32[]{:S(2)}) copy-start(bf16[768,2048]{1,0:T(8,128)(2,1)} %get-tuple-element.49) | copy-start | bytes 9437188
  250.4 6.1 %copy-start.29 = (f32[8,192]{1,0:T(8,128)S(1)}, f32[8,192]{1,0:T(8,128)}, u32[]{:S(2)}) copy-start(f32[8,192]{1,0:T(8,128)} %get-tuple-element.51) | copy-start | bytes 18436
  250.4 6.2 %copy-start.32 = (f32[32]{0:T(128)S(1)}, f32[32]{0:T(128)}, u32[]{:S(2)}) copy-start(f32[32]{0:T(128)} %mul.263) | copy-start | bytes 388
  250.4 6.3 %copy-start.22 = (bf16[1,32,24]{2,0,1:T(2,128)(2,1)S(1)}, bf16[1,32,24]{2,0,1:T(2,128)(2,1)}, u32[]{:S(2)}) copy-start(bf16[1,32,24]{2,0,1:T(2,128)(2,1)} %concatenate.46) | copy-start | bytes 4612
  250.4 6.5 %copy-start.33 = (bf16[16]{0:T(256)(128)(2,1)S(1)}, bf16[16]{0:T(256)(128)(2,1)}, u32[]{:S(2)}) copy-start(bf16[16]{0:T(256)(128)(2,1)} %pad.18.clone) | copy-start | bytes 100
  255.0 2.7 copy-start.14
  257.7 6.4 %copy-start.12 = (bf16[256,3072]{1,0:T(8,128)(2,1)S(1)}, bf16[256,3072]{1,0:T(8,128)(2,1)}, u32[]{:S(2)}) copy-start(bf16[256,3072]{1,0:T(8,128)(2,1)} %copy-done.11) | copy-start | bytes 4718596
  257.7 6.4 %copy-start.26 = (f32[256]{0:T(256)S(1)}, f32[256]{0:T(256)}, u32[]{:S(2)}) copy-start(f32[256]{0:T(256)} %copy-done.25) | copy-start | bytes 3076
  264.1 3.8 %copy-start.15 = (f32[768,192]{1,0:T(8,128)S(1)}, f32[768,192]{1,0:T(8,128)}, u32[]{:S(2)}) copy-start(f32[768,192]{1,0:T(8,128)} %fusion.42) | copy-start | bytes 1769476
  268.4 3.1 copy-start.24
  271.5 3.0 copy-start.7
  271.5 3.0 copy-start.10
  354.8 8.1 %copy-start.16 = (bf16[2,128,768]{2,1,0:T(8,128)(2,1)S(1)}, bf16[2,128,768]{2,1,0:T(8,128)(2,1)}, u32[]{:S(2)}) copy-start(bf16[2,128,768]{2,1,0:T(8,128)(2,1)} %get-tuple-element.105) | copy-start | bytes 1179652
  354.8 8.9 %copy-start.21 = (f32[24,768]{1,0:T(8,128)S(1)}, f32[24,768]{1,0:T(8,128)}, u32[]{:S(2)}) copy-start(f32[24,768]{1,0:T(8,128)} %get-tuple-element.108) | copy-start | bytes 221188
  354.8 9.5 %copy-start.20 = (f32[24,768]{1,0:T(8,128)S(1)}, f32[24,768]{1,0:T(8,128)}, u32[]{:S(2)}) copy-start(f32[24,768]{1,0:T(8,128)} %get-tuple-element.109) | copy-start | bytes 221188
  354.8 10.1 %copy-start.18 = (f32[24,3072]{1,0:T(8,128)S(1)}, f32[24,3072]{1,0:T(8,128)}, u32[]{:S(2)}) copy-start(f32[24,3072]{1,0:T(8,128)} %get-tuple-element.110) | copy-start | bytes 884740
  354.8 10.8 %copy-start.17 = (f32[96,768]{1,0:T(8,128)S(1)}, f32[96,768]{1,0:T(8,128)}, u32[]{:S(2)}) copy-start(f32[96,768]{1,0:T(8,128)} %get-tuple-element.111) | copy-start | bytes 884740
